TPU v7x, 32 devices: a whole 2x2x4 slice. The times are simulated.
32 devices in a mesh: gx: 4 (over y, x), gy: 8 (over z, core).
Axes of the slice: x: 2, y: 2, z: 4, core: 2. Of those that a mesh axis runs over, the one named last changes fastest.
Arguments:
- operator_t: bfloat16 [64, 512, 2432], P('gx', 'gy'), may hold values from -0.046875 to 0.046875
- data_columns: bfloat16 [2432, 384], P(('gx', 'gy')), may hold values from -6 to 6
- noise_var: float32 [2432], P(('gx', 'gy')), may hold values from 0.05 to 0.5
- class_map: int32 [64, 512], P('gx', 'gy'), may hold values from 0 to 15
- diffusion_table: float32 [16], replicated, may hold values from 0.5 to 4
- kappa_table: float32 [16], replicated, may hold values from 0.02 to 0.3
Outputs:
- hessian_block: float32 [2432, 384], P(('gx', 'gy'))
- prior_field: float32 [64, 512, 384], P('gx', 'gy')
All inputs are finite; a program needn't handle non-finite values.
Results may differ from a plain program's by a relative error of at most 0.0003.
Values may be sent and summed in bfloat16 or wider, within the bound.
A program may use at most 64 MiB of HBM per device.

v0:
```python
import functools
import jax
import jax.numpy as jnp
from jax import lax
from jax.experimental import pallas as pl
from jax.experimental.pallas import tpu as pltpu
from jax.sharding import PartitionSpec as P

ITERS = 8
LANES = 128
LEVELS = 32767.0
MESH = pl.DeviceIdType.MESH


def up8(n):
    return -(-n // 8) * 8


def remote(src, dst, send, recv, device):
    return pltpu.make_async_remote_copy(
        src_ref=src, dst_ref=dst, send_sem=send, recv_sem=recv, device_id=device, device_id_type=MESH
    )


def top_of(value, axes):
    return jnp.maximum(jnp.max(jnp.abs(value), axis=axes, keepdims=True), 1e-30)


def coded(value, top):
    return jnp.round(value * (LEVELS / top)).astype(jnp.int32).astype(jnp.int16)


def decoded(codes, scale):
    return codes.astype(jnp.int32).astype(jnp.float32) * scale


def block_kernel(
    dims, counts, start_row, H,
    mine, classes, diffusion_table, kappa_table, operator_hbm,
    out, prior,
    operator, full, stage, data, near_classes, coef, inverse,
    s, u, v, q_out, q_scale, q_in, q_in_scale, smooth,
    flat, wide, sib_in, xy_q, xy_c, xy_r, xy_f, z_q, z_c, z_r, z_f, own,
    op_sem, cls_s, cls_r, gz_s, gz_r, gx_s, gx_r, gs_s, gs_r,
    hq_s, hq_r, hc_s, hc_r, he_s, he_r, hk_s, hk_r,
    rs_s, rs_r, rq_s, rq_r, rc_s, rc_r, zq_s, zq_r, zc_s, zc_r,
):
    Y, X, Z = dims
    m = ITERS
    chunks = s.shape[0]
    rows, cols = prior.shape[0], prior.shape[1]
    count = mine.shape[0]
    pair = 2 * count
    chips = Y * X * Z
    count_x, count_y = counts
    gx, gy = lax.axis_index("gx"), lax.axis_index("gy")
    y, x, z, me = gx // X, gx % X, gy // 2, gy % 2
    offsets = [(dy, dx) for dy in range(Y) for dx in range(X)][1:]
    offsets.sort(key=lambda d: (d[0] != 0) + (d[1] != 0))

    def device(y=y, x=x, z=z, core=me):
        return (y * X + x, z * 2 + core)

    sib = device(core=1 - me)
    z_peers = [device(z=(z + d) % Z) for d in range(1, Z)]
    xy_peers = [device(y=(y + dy) % Y, x=(x + dx) % X) for dy, dx in offsets]
    around = [(dr, dc) for dr in (-1, 0, 1) for dc in (-1, 0, 1) if (dr, dc) != (0, 0)]

    def exists(dr, dc):
        has = None
        for d, at, n in ((dr, gx, count_x), (dc, gy, count_y)):
            if d:
                ok = at > 0 if d < 0 else at < n - 1
                has = ok if has is None else has & ok
        return has

    def lanes(g):
        return pl.ds(g * LANES, LANES)

    pending = []

    def send(src, dst, sends, recvs, peer):
        copy = remote(src, dst, sends, recvs, peer)
        copy.start()
        pending.append((None, copy))

    def send_if(has, src, dst, sends, recvs, peer):
        copy = remote(src, dst, sends, recvs, peer)

        @pl.when(has)
        def _():
            copy.start()

        pending.append((has, copy))

    def arrived(ref, sends, recvs):
        remote(ref, ref, sends, recvs, sib).wait_recv()

    load = pltpu.make_async_copy(operator_hbm, operator, op_sem)
    load.start()
    for g in range(chunks):
        full[g, y, x, me, z] = mine[:, g * LANES : (g + 1) * LANES]

    wide_rows, wide_cols = rows + 2 * m, cols + 2 * m
    for (dr, dc), where in (
        ((-1, 0), (pl.ds(0, m), pl.ds(0, wide_cols))),
        ((1, 0), (pl.ds(m + rows, m), pl.ds(0, wide_cols))),
        ((0, -1), (pl.ds(0, wide_rows), pl.ds(0, m))),
        ((0, 1), (pl.ds(0, wide_rows), pl.ds(m + cols, m))),
    ):

        @pl.when(jnp.logical_not(exists(dr, dc)))
        def _():
            for g in range(chunks):
                s[g, where[0], where[1]] = jnp.zeros(
                    (where[0].size, where[1].size, LANES), jnp.float32
                )

    ready = pltpu.get_barrier_semaphore()
    for peer in [sib, *z_peers, *xy_peers]:
        pl.semaphore_signal(ready, inc=1, device_id=peer, device_id_type=MESH)
    total = 1 + len(z_peers) + len(xy_peers)
    for dr, dc in around:

        @pl.when(exists(dr, dc))
        def _():
            pl.semaphore_signal(
                ready, inc=1, device_id=(gx + dr, gy + dc), device_id_type=MESH
            )

        total = total + jnp.where(exists(dr, dc), 1, 0)
    pl.semaphore_wait(ready, total)

    for i, (dr, dc) in enumerate(around):
        send_if(
            exists(dr, dc), classes, near_classes.at[7 - i], cls_s.at[i], cls_r.at[7 - i],
            (gx + dr, gy + dc),
        )
    for g in range(chunks):
        home = full.at[g, y, x, me, z]
        for d in range(1, Z):
            send(home, home, gz_s.at[g, d - 1], gz_r.at[g, d - 1], z_peers[d - 1])
        for j, peer in enumerate(xy_peers):
            send(home, home, gx_s.at[g, 0, j], gx_r.at[g, 0, j], peer)

    for i, (dr, dc) in enumerate(around):
        has = exists(dr, dc)

        @pl.when(has)
        def _():
            arrived(near_classes.at[i], cls_s.at[i], cls_r.at[i])

        @pl.when(jnp.logical_not(has))
        def _():
            near_classes[i] = jnp.full((rows, LANES), -1, jnp.int32)

    reach = m + 1
    lane = lax.broadcasted_iota(jnp.int32, (rows, LANES), 1)
    window = []
    for dr in (-1, 0, 1):
        west, centre, east = [
            near_classes[around.index((dr, dc))] if (dr, dc) != (0, 0) else classes[...]
            for dc in (-1, 0, 1)
        ]
        west = pltpu.roll(west, LANES - (cols - reach), 1)
        centre = pltpu.roll(centre, reach, 1)
        east = pltpu.roll(east, reach + cols, 1)
        line = jnp.where(lane < reach, west, jnp.where(lane < reach + cols, centre, east))
        window.append(jnp.where(lane < 2 * reach + cols, line, -1))
    window = jnp.concatenate(window, axis=0)
    tall = 3 * rows
    diffusion = jnp.zeros((tall, LANES), jnp.float32)
    reaction = jnp.zeros((tall, LANES), jnp.float32)
    for k in range(diffusion_table.shape[0]):
        hit = window == k
        diffusion = jnp.where(hit, diffusion_table[k], diffusion)
        reaction = jnp.where(hit, kappa_table[k], reaction)
    inside = window >= 0
    weights = [
        0.5 * (diffusion + pltpu.roll(diffusion, shift, axis))
        for shift, axis in ((1, 0), (tall - 1, 0), (1, 1), (LANES - 1, 1))
    ]
    divisor = jnp.where(
        inside, reaction + weights[0] + weights[1] + weights[2] + weights[3], 1.0
    )

    def upright(values):
        values = pltpu.roll(values, LANES - 1, 1)[rows - m : rows - m + wide_rows]
        padded = jnp.concatenate(
            [values, jnp.zeros((LANES - wide_rows, LANES), jnp.float32)], axis=0
        )
        return padded.T

    for i, w in enumerate(weights):
        turned = upright(jnp.where(inside, w / divisor, 0.0))
        for r in range(wide_rows):
            coef[i, r] = jnp.broadcast_to(turned[:wide_cols, r : r + 1], (wide_cols, LANES))
    turned = upright(1.0 / divisor)
    for r in range(rows):
        inverse[r] = jnp.broadcast_to(turned[m : m + cols, m + r : m + r + 1], (cols, LANES))

    def held(g, d, core=me):
        return full.at[g, y, x, core, (z - d) % Z]

    def to_sibling(g, j):
        dy, dx = ([(0, 0)] + offsets)[j]
        group = full.at[g, (y - dy) % Y, (x - dx) % X, me]
        send(group, group, gs_s.at[g, j], gs_r.at[g, j], sib)

    def gather_z(g):
        for d in range(1, Z):
            block = held(g, d)
            arrived(block, gz_s.at[g, d - 1], gz_r.at[g, d - 1])
            for j, peer in enumerate(xy_peers):
                send(block, block, gx_s.at[g, d, j], gx_r.at[g, d, j], peer)
        to_sibling(g, 0)

    def gather_xy(g):
        for j, (dy, dx) in enumerate(offsets):
            for d in range(Z):
                block = full.at[g, (y - dy) % Y, (x - dx) % X, me, (z - d) % Z]
                arrived(block, gx_s.at[g, d, j], gx_r.at[g, d, j])
            to_sibling(g, j + 1)

    def sources(g):
        for j, (dy, dx) in enumerate([(0, 0)] + offsets):
            group = full.at[g, (y - dy) % Y, (x - dx) % X, 1 - me]
            arrived(group, gs_s.at[g, j], gs_r.at[g, j])
        number = 0
        for yy in range(Y):
            for xx in range(X):
                for zz in range(Z):
                    for core in (0, 1):
                        stage[pl.ds(number * count, count), :] = full[
                            g, yy, xx, core, zz
                        ].astype(jnp.float32)
                        number += 1
        data[...] = stage[...].astype(jnp.bfloat16)
        source = jnp.dot(operator[...], data[...], preferred_element_type=jnp.float32)
        tile = source.reshape(rows, cols, LANES) * inverse[...]
        s[g, pl.ds(m, rows), pl.ds(m, cols)] = tile
        top = top_of(tile, (0, 1))
        q_out[g] = coded(tile, top)
        q_scale[g] = jnp.broadcast_to(top[0] * (1.0 / LEVELS), (8, LANES))

    north, south, west, east = (-1, 0), (1, 0), (0, -1), (0, 1)

    def peer_of(d):
        return (gx + d[0], gy + d[1])

    def halo_send(g):
        for i, (d, at) in enumerate(((north, 0), (south, rows - m))):
            has = exists(*d)
            send_if(
                has, q_out.at[g, pl.ds(at, m)], q_in.at[g, i], hq_s.at[g, i], hq_r.at[g, i],
                peer_of(d),
            )
            send_if(
                has, q_scale.at[g], q_in_scale.at[g, i], hc_s.at[g, i], hc_r.at[g, i], peer_of(d)
            )
        inner = pl.ds(m, rows)
        for i, (d, src, dst) in enumerate(((west, m, m + cols), (east, cols, 0))):
            send_if(
                exists(*d), s.at[g, inner, pl.ds(src, m)], s.at[g, inner, pl.ds(dst, m)],
                he_s.at[g, i], he_r.at[g, i], peer_of(d),
            )

    def halo_recv(g):
        for i, (d, at) in enumerate(((south, m + rows), (north, 0))):

            @pl.when(exists(*d))
            def _():
                arrived(q_in.at[g, i], hq_s.at[g, i], hq_r.at[g, i])
                arrived(q_in_scale.at[g, i], hc_s.at[g, i], hc_r.at[g, i])
                s[g, pl.ds(at, m), pl.ds(m, cols)] = decoded(
                    q_in[g, i], q_in_scale[g, i][:1][None]
                )

        for i, (d, src, dst) in enumerate(((west, m, m + cols), (east, cols, 0))):
            for k, at in enumerate((0, m + rows)):
                send_if(
                    exists(*d), s.at[g, pl.ds(at, m), pl.ds(src, m)],
                    s.at[g, pl.ds(at, m), pl.ds(dst, m)],
                    hk_s.at[g, i, k], hk_r.at[g, i, k], peer_of(d),
                )

    def halo_sides(g):
        for i, (d, dst) in enumerate(((east, m + cols), (west, 0))):

            @pl.when(exists(*d))
            def _():
                block = s.at[g, pl.ds(m, rows), pl.ds(dst, m)]
                arrived(block, he_s.at[g, i], he_r.at[g, i])
                for k, at in enumerate((0, m + rows)):
                    block = s.at[g, pl.ds(at, m), pl.ds(dst, m)]
                    arrived(block, hk_s.at[g, i, k], hk_r.at[g, i, k])

    def sweeps(g):
        turns = [u, v]
        fixed = s.at[g]
        for step in range(1, m + 1):
            old = fixed if step == 1 else turns[step % 2]
            new = turns[(step + 1) % 2]
            last = step == m

            @pl.loop(step, wide_rows - step)
            def _(r):
                centre = old[r]
                value = fixed[r] + coef[0, r] * old[r - 1]
                value = value + coef[1, r] * old[r + 1]
                value = value + coef[2, r] * pltpu.roll(centre, 1, 0)
                value = value + coef[3, r] * pltpu.roll(centre, wide_cols - 1, 0)
                if last:
                    done = value[m : m + cols]
                    prior[r - m, :, lanes(g)] = done
                    at = pl.multiple_of((r - m) * cols, cols)
                    smooth[pl.ds(at, cols), :] = done.astype(jnp.bfloat16)
                else:
                    new[r] = value

    mine_rows = pl.ds(pl.multiple_of(me * start_row, 8), H)
    other_rows = pl.ds(pl.multiple_of((1 - me) * start_row, 8), H)
    groups = [*offsets, (0, 0)]

    def group_at(j):
        dy, dx = groups[j]
        return ((y + dy) % Y) * X + (x + dx) % X

    def forward(g):
        partial = lax.dot_general(
            operator[...], smooth[...], (((0,), (0,)), ((), ())),
            preferred_element_type=jnp.float32,
        )
        if pair % 8 == 0:
            wide[g] = partial.reshape(Y * X, Z, pair, LANES)
        else:
            flat[...] = partial
            for k in range(chips):
                wide[g, k // Z, k % Z, pl.ds(0, pair)] = flat[pl.ds(k * pair, pair)]
                rest = wide.shape[3] - pair
                wide[g, k // Z, k % Z, pl.ds(pair, rest)] = jnp.zeros((rest, LANES), jnp.float32)
        for j in range(len(groups)):
            k = group_at(j)
            send(
                wide.at[g, k, :, other_rows], sib_in.at[g, k], rs_s.at[g, j], rs_r.at[g, j], sib
            )

    def pair_sum(g, j, zz):
        k = group_at(j)
        return wide[g, k, zz, mine_rows] + sib_in[g, k, zz]

    def scatter_xy(g):
        for j, peer in enumerate(xy_peers):
            k = group_at(j)
            arrived(sib_in.at[g, k], rs_s.at[g, j], rs_r.at[g, j])
            for zz in range(Z):
                value = pair_sum(g, j, zz)
                top = top_of(value, (0,))
                xy_q[g, j, zz] = coded(value, top)
                xy_c[g, j, pl.ds(zz, 1)] = top * (1.0 / LEVELS)
            send(xy_q.at[g, j], xy_r.at[g, j], rq_s.at[g, j], rq_r.at[g, j], peer)
            send(xy_c.at[g, j], xy_f.at[g, j], rc_s.at[g, j], rc_r.at[g, j], peer)

    def scatter_z(g):
        j = len(xy_peers)
        arrived(sib_in.at[g, group_at(j)], rs_s.at[g, j], rs_r.at[g, j])
        for i in range(j):
            arrived(xy_r.at[g, i], rq_s.at[g, i], rq_r.at[g, i])
            arrived(xy_f.at[g, i], rc_s.at[g, i], rc_r.at[g, i])

        def summed(zz):
            value = pair_sum(g, j, zz)
            for i in range(j):
                value = value + decoded(xy_r[g, i, zz], xy_f[g, i, pl.ds(zz, 1)])
            return value

        for d in range(1, Z):
            value = summed((z + d) % Z)
            top = top_of(value, (0,))
            z_q[g, d - 1] = coded(value, top)
            z_c[g, d - 1] = jnp.broadcast_to(top * (1.0 / LEVELS), (8, LANES))
            send(z_q.at[g, d - 1], z_r.at[g, d - 1], zq_s.at[g, d - 1], zq_r.at[g, d - 1], z_peers[d - 1])
            send(z_c.at[g, d - 1], z_f.at[g, d - 1], zc_s.at[g, d - 1], zc_r.at[g, d - 1], z_peers[d - 1])
        own[g] = summed(z)

    def scatter_end(g):
        value = own[g]
        for d in range(1, Z):
            arrived(z_r.at[g, d - 1], zq_s.at[g, d - 1], zq_r.at[g, d - 1])
            arrived(z_f.at[g, d - 1], zc_s.at[g, d - 1], zc_r.at[g, d - 1])
            value = value + decoded(z_r[g, d - 1], z_f[g, d - 1][:1])
        out[:, lanes(g)] = value

    for g in range(chunks):
        gather_z(g)
    load.wait()
    for g in range(chunks):
        gather_xy(g)
        if g == chunks - 1 and g:
            halo_recv(0)
        sources(g)
        halo_send(g)
    if chunks == 1:
        halo_recv(0)
    for g in range(chunks):
        halo_sides(g)
        sweeps(g)
        if g + 1 < chunks:
            halo_recv(g + 1)
        if g >= 2:
            scatter_z(g - 2)
        if g >= 1:
            scatter_xy(g - 1)
        forward(g)
    if chunks >= 2:
        scatter_z(chunks - 2)
    scatter_xy(chunks - 1)
    for g in range(chunks - 1):
        scatter_end(g)
    scatter_z(chunks - 1)
    scatter_end(chunks - 1)
    for has, copy in pending:
        if has is None:
            copy.wait_send()
        else:

            @pl.when(has)
            def _():
                copy.wait_send()


def local(operator_t, data_columns, noise_var, class_map, diffusion_table, kappa_table):
    rows, cols, data_rows = operator_t.shape
    count, width = data_columns.shape
    gx_size, gy_size = lax.axis_size("gx"), lax.axis_size("gy")
    X = 2
    Y, Z = gx_size // X, gy_size // 2
    chips = Y * X * Z
    points = rows * cols
    chunks = width // LANES
    m = ITERS
    start = count // 8 * 8
    H = max(up8(count), up8(2 * count) - start)
    tall = max(start + H, 2 * count)
    f32, bf16, i16, i32 = jnp.float32, jnp.bfloat16, jnp.int16, jnp.int32
    peers, zs = Y * X - 1, max(Z - 1, 1)

    def vmem(*shape, kind=f32):
        return pltpu.VMEM(shape, kind)

    def sems(*shape):
        return [pltpu.SemaphoreType.DMA(shape)] * 2

    field = (rows + 2 * m, cols + 2 * m)
    even = 2 * count % 8 == 0
    scratch = [
        vmem(points, data_rows, kind=bf16),
        vmem(chunks, Y, X, 2, Z, count, LANES, kind=bf16),
        vmem(data_rows, LANES),
        vmem(data_rows, LANES, kind=bf16),
        vmem(8, rows, LANES, kind=i32),
        vmem(4, *field, LANES),
        vmem(rows, cols, LANES),
        vmem(chunks, *field, LANES),
        vmem(*field, LANES),
        vmem(*field, LANES),
        vmem(chunks, rows, cols, LANES, kind=i16),
        vmem(chunks, 8, LANES),
        vmem(chunks, 2, m, cols, LANES, kind=i16),
        vmem(chunks, 2, 8, LANES),
        vmem(points, LANES, kind=bf16),
        vmem(*((8,) if even else (data_rows,)), LANES),
        vmem(chunks, Y * X, Z, tall, LANES),
        vmem(chunks, Y * X, Z, H, LANES),
        vmem(chunks, peers, Z, H, LANES, kind=i16),
        vmem(chunks, peers, Z, LANES),
        vmem(chunks, peers, Z, H, LANES, kind=i16),
        vmem(chunks, peers, Z, LANES),
        vmem(chunks, zs, H, LANES, kind=i16),
        vmem(chunks, zs, 8, LANES),
        vmem(chunks, zs, H, LANES, kind=i16),
        vmem(chunks, zs, 8, LANES),
        vmem(chunks, H, LANES),
        pltpu.SemaphoreType.DMA,
        *sems(8),
        *sems(chunks, zs),
        *sems(chunks, Z, peers),
        *sems(chunks, peers + 1),
        *sems(chunks, 2),
        *sems(chunks, 2),
        *sems(chunks, 2),
        *sems(chunks, 2, 2),
        *sems(chunks, peers + 1),
        *sems(chunks, peers),
        *sems(chunks, peers),
        *sems(chunks, zs),
        *sems(chunks, zs),
    ]
    block = pl.BlockSpec(memory_space=pltpu.VMEM)
    table = pl.BlockSpec(memory_space=pltpu.SMEM)
    classes = jnp.pad(class_map, ((0, 0), (0, LANES - cols)), constant_values=-1)
    out, prior = pl.pallas_call(
        functools.partial(block_kernel, (Y, X, Z), (gx_size, gy_size), start, H),
        out_shape=(
            jax.ShapeDtypeStruct((H, width), f32),
            jax.ShapeDtypeStruct((rows, cols, width), f32),
        ),
        in_specs=[block, block, table, table, pl.BlockSpec(memory_space=pl.ANY)],
        out_specs=(block, block),
        scratch_shapes=scratch,
        compiler_params=pltpu.CompilerParams(
            collective_id=0, has_side_effects=True, vmem_limit_bytes=60 << 20
        ),
    )(data_columns, classes, diffusion_table, kappa_table, operator_t.reshape(points, data_rows))
    core = lax.axis_index("gy") % 2
    forward = jnp.where(core == 0, out[:count], out[count - start : 2 * count - start])
    return (forward + noise_var[:, None] * data_columns.astype(f32), prior)


def solution(mesh):
    placed = (P("gx", "gy", None), P(("gx", "gy"), None), P(("gx", "gy")), P("gx", "gy"), P(), P())
    return jax.shard_map(
        local,
        mesh=mesh,
        in_specs=placed,
        out_specs=(P(("gx", "gy"), None), P("gx", "gy", None)),
        check_vma=False,
    )
```

profile of v0, /device:TPU:0, one launch (start us, length us, event | category | flops | bytes accessed | tf_op | source)
XLA Modules:
  0.0 77.3 jit_solution(16183350711972974140)
XLA Ops:
  0.6 1.3 %pad.4.classes = s32[16,128]{1,0:T(8,128)} pad(s32[16,64]{1,0:T(8,128)} %param.9, s32[]{:T(128)} %constant.19.clone.1), padding=0_0x0_64 | pad | bytes 12292 | tf_op jit(solution)/shard_map/jit(_pad)/pad | solution.py:501
  1.9 0.0 copy-start
  1.9 0.0 copy-start.1
  1.9 70.9 %shard_map.77 = (f32[80,384]{1,0:T(8,128)}, f32[16,64,384]{2,1,0:T(8,128)}) custom-call(bf16[76,384]{1,0:T(8,128)(2,1)} %mine.1, s32[16,128]{1,0:T(8,128)} %pad.4.classes, f32[16]{0:T(128)} %diffusion_table.1, f32[16]{0:T(128)} %kappa_table.1, bf16[1024,2432]{1,0:T(8,128)(2,1)} %bitcast.1), custom_call_target="tpu_custom_call" | custom-call | tf_op jit(solution)/shard_map/pallas_call | solution.py:502
  72.9 0.0 copy-done
  72.9 0.0 copy-done.1
  72.9 1.7 %multiply_add_fusion = f32[76,384]{1,0:T(8,128)} fusion(bf16[76,384]{1,0:T(8,128)(2,1)S(1)} %copy-done, f32[80,384]{1,0:T(8,128)} %get-tuple-element.4, f32[76]{0:T(128)S(1)} %copy-done.1, pred[]{:T(512)S(6)} %eq.5), kind=kLoop, calls=%fused_computation | loop fusion | flops 116736 | bytes 408881 | tf_op jit(solution)/shard_map/add | solution.py:517
  74.6 2.7 %copy.9 = f32[16,64,384]{2,1,0:T(8,128)} copy(f32[16,64,384]{2,1,0:T(8,128)} %get-tuple-element.9) | data formatting | bytes 3145728
Async XLA Ops:
  1.9 71.0 %copy-start = (bf16[76,384]{1,0:T(8,128)(2,1)S(1)}, bf16[76,384]{1,0:T(8,128)(2,1)}, u32[]{:S(2)}) copy-start(bf16[76,384]{1,0:T(8,128)(2,1)} %mine.1) | copy-start | bytes 175108
  1.9 71.0 %copy-start.1 = (f32[76]{0:T(128)S(1)}, f32[76]{0:T(128)}, u32[]{:S(2)}) copy-start(f32[76]{0:T(128)} %param.8) | copy-start | bytes 916
where the time goes:
time: 77.6 us; the launch traced here: 77.3 us
  Pallas kernels  70.9 us (91%)
  local copies, waits for them, and re-layouts  4.01 us (5%)
  other arithmetic  1.71 us (2%)
    pallas_call x1, Pallas kernels, local(): pl.pallas_call(functools.partial(block_kernel, (Y, X, Z), (gx_size, gy_si...  70.9 us
    unnamed x5, local copies, waits for them, and re-layouts  2.71 us
    add x1, other arithmetic, local(): return (forward + noise_var[:, None] * data_columns.astype(f32), prior)  1.71 us

commit v1 on v0

v1 whole, which is shorter than its diff:
```python
import functools
import jax
import jax.numpy as jnp
from jax import lax
from jax.experimental import pallas as pl
from jax.experimental.pallas import tpu as pltpu
from jax.sharding import PartitionSpec as P

ITERS = 8
LANES = 128
LEVELS = 32767.0
MESH = pl.DeviceIdType.MESH


def up8(n):
    return -(-n // 8) * 8


def remote(src, dst, send, recv, device):
    return pltpu.make_async_remote_copy(
        src_ref=src, dst_ref=dst, send_sem=send, recv_sem=recv, device_id=device, device_id_type=MESH
    )


def top_of(value, axes):
    return jnp.maximum(jnp.max(jnp.abs(value), axis=axes, keepdims=True), 1e-30)


def coded(value, top):
    return jnp.round(value * (LEVELS / top)).astype(jnp.int32).astype(jnp.int16)


def decoded(codes, scale):
    return codes.astype(jnp.int32).astype(jnp.float32) * scale


def block_kernel(
    dims, counts, start_row, H,
    mine, class_map, diffusion_table, kappa_table, operator_hbm,
    out, prior,
    operator, classes, full, stage, data, near_classes, coef, inverse,
    s, u, v, q_out, q_scale, q_in, q_in_scale, smooth,
    flat, wide, sib_in, xy_q, xy_c, xy_r, xy_f, z_q, z_c, z_r, z_f, own,
    op_sem, own_sem, cls_s, cls_r, gz_s, gz_r, gx_s, gx_r, gs_s, gs_r,
    hq_s, hq_r, hc_s, hc_r, he_s, he_r, hk_s, hk_r,
    rs_s, rs_r, rq_s, rq_r, rc_s, rc_r, zq_s, zq_r, zc_s, zc_r,
):
    Y, X, Z = dims
    m = ITERS
    chunks = s.shape[0]
    rows, cols = prior.shape[0], prior.shape[1]
    count = mine.shape[0]
    pair = 2 * count
    chips = Y * X * Z
    count_x, count_y = counts
    gx, gy = lax.axis_index("gx"), lax.axis_index("gy")
    y, x, z, me = gx // X, gx % X, gy // 2, gy % 2
    offsets = [(dy, dx) for dy in range(Y) for dx in range(X)][1:]
    offsets.sort(key=lambda d: (d[0] != 0) + (d[1] != 0))

    def device(y=y, x=x, z=z, core=me):
        return (y * X + x, z * 2 + core)

    sib = device(core=1 - me)
    z_peers = [device(z=(z + d) % Z) for d in range(1, Z)]
    xy_peers = [device(y=(y + dy) % Y, x=(x + dx) % X) for dy, dx in offsets]
    def exists(dr, dc):
        has = None
        for d, at, n in ((dr, gx, count_x), (dc, gy, count_y)):
            if d:
                ok = at > 0 if d < 0 else at < n - 1
                has = ok if has is None else has & ok
        return has

    def lanes(g):
        return pl.ds(g * LANES, LANES)

    pending = []

    def send(src, dst, sends, recvs, peer):
        copy = remote(src, dst, sends, recvs, peer)
        copy.start()
        pending.append((None, copy))

    def send_if(has, src, dst, sends, recvs, peer):
        copy = remote(src, dst, sends, recvs, peer)

        @pl.when(has)
        def _():
            copy.start()

        pending.append((has, copy))

    def arrived(ref, sends, recvs):
        remote(ref, ref, sends, recvs, sib).wait_recv()

    load = pltpu.make_async_copy(operator_hbm, operator, op_sem)
    load.start()
    homes = [
        pltpu.make_async_copy(mine.at[:, lanes(g)], full.at[g, y, x, me, z], own_sem.at[g])
        for g in range(chunks)
    ]
    for copy in homes:
        copy.start()
    classes[...] = jnp.full(classes.shape, -1, jnp.int32)
    classes[1, :, pl.ds(0, cols)] = class_map[...]

    wide_rows, wide_cols = rows + 2 * m, cols + 2 * m
    for (dr, dc), where in (
        ((-1, 0), (pl.ds(0, m), pl.ds(0, wide_cols))),
        ((1, 0), (pl.ds(m + rows, m), pl.ds(0, wide_cols))),
        ((0, -1), (pl.ds(0, wide_rows), pl.ds(0, m))),
        ((0, 1), (pl.ds(0, wide_rows), pl.ds(m + cols, m))),
    ):

        @pl.when(jnp.logical_not(exists(dr, dc)))
        def _():
            for g in range(chunks):
                s[g, where[0], where[1]] = jnp.zeros(
                    (where[0].size, where[1].size, LANES), jnp.float32
                )

    ready = pltpu.get_barrier_semaphore()
    for peer in [sib, *z_peers, *xy_peers]:
        pl.semaphore_signal(ready, inc=1, device_id=peer, device_id_type=MESH)
    beyond = gy + 2 * me - 1
    has_beyond = (beyond >= 0) & (beyond < count_y)

    @pl.when(has_beyond)
    def _():
        pl.semaphore_signal(ready, inc=1, device_id=(gx, beyond), device_id_type=MESH)

    pl.semaphore_wait(
        ready, 1 + len(z_peers) + len(xy_peers) + jnp.where(has_beyond, 1, 0)
    )

    north, south, west, east = (-1, 0), (1, 0), (0, -1), (0, 1)

    def peer_of(d):
        return (gx + d[0], gy + d[1])

    def class_sides_send():
        for i, (d, slot) in enumerate(((west, 2), (east, 0))):
            send_if(
                exists(*d), classes.at[1], classes.at[slot], cls_s.at[i], cls_r.at[i], peer_of(d)
            )

    def class_sides():
        for i, (d, slot) in enumerate(((east, 2), (west, 0))):

            @pl.when(exists(*d))
            def _():
                arrived(classes.at[slot], cls_s.at[i], cls_r.at[i])

        for i, (d, slot) in enumerate(((north, 1), (south, 0))):
            send_if(
                exists(*d), classes, near_classes.at[slot], cls_s.at[2 + i], cls_r.at[2 + i],
                peer_of(d),
            )

    class_sides_send()
    for copy in homes:
        copy.wait()
    for g in range(chunks):
        home = full.at[g, y, x, me, z]
        for d in range(1, Z):
            send(home, home, gz_s.at[g, d - 1], gz_r.at[g, d - 1], z_peers[d - 1])
        for j, peer in enumerate(xy_peers):
            send(home, home, gx_s.at[g, 0, j], gx_r.at[g, 0, j], peer)

    def coefficients():
        for i, (d, slot) in enumerate(((south, 1), (north, 0))):

            @pl.when(exists(*d))
            def _():
                arrived(near_classes.at[slot], cls_s.at[2 + i], cls_r.at[2 + i])

            @pl.when(jnp.logical_not(exists(*d)))
            def _():
                near_classes[slot] = jnp.full(near_classes.shape[1:], -1, jnp.int32)

        reach = m + 1
        lane = lax.broadcasted_iota(jnp.int32, (rows, LANES), 1)
        window = []
        for dr in (-1, 0, 1):
            held_at = (near_classes.at[0], classes, near_classes.at[1])[dr + 1]
            left = pltpu.roll(held_at[0], LANES - (cols - reach), 1)
            centre = pltpu.roll(held_at[1], reach, 1)
            right = pltpu.roll(held_at[2], reach + cols, 1)
            line = jnp.where(lane < reach, left, jnp.where(lane < reach + cols, centre, right))
            window.append(jnp.where(lane < 2 * reach + cols, line, -1))
        window = jnp.concatenate(window, axis=0)
        tall = 3 * rows
        diffusion = jnp.zeros((tall, LANES), jnp.float32)
        reaction = jnp.zeros((tall, LANES), jnp.float32)
        for k in range(diffusion_table.shape[0]):
            hit = window == k
            diffusion = jnp.where(hit, diffusion_table[k], diffusion)
            reaction = jnp.where(hit, kappa_table[k], reaction)
        inside = window >= 0
        weights = [
            0.5 * (diffusion + pltpu.roll(diffusion, shift, axis))
            for shift, axis in ((1, 0), (tall - 1, 0), (1, 1), (LANES - 1, 1))
        ]
        divisor = jnp.where(
            inside, reaction + weights[0] + weights[1] + weights[2] + weights[3], 1.0
        )

        def upright(values):
            values = pltpu.roll(values, LANES - 1, 1)[rows - m : rows - m + wide_rows]
            padded = jnp.concatenate(
                [values, jnp.zeros((LANES - wide_rows, LANES), jnp.float32)], axis=0
            )
            return padded.T

        for i, w in enumerate(weights):
            turned = upright(jnp.where(inside, w / divisor, 0.0))
            for r in range(wide_rows):
                coef[i, r] = jnp.broadcast_to(turned[:wide_cols, r : r + 1], (wide_cols, LANES))
        turned = upright(1.0 / divisor)
        for r in range(rows):
            inverse[r] = jnp.broadcast_to(turned[m : m + cols, m + r : m + r + 1], (cols, LANES))


    def held(g, d, core=me):
        return full.at[g, y, x, core, (z - d) % Z]

    def to_sibling(g, j):
        dy, dx = ([(0, 0)] + offsets)[j]
        group = full.at[g, (y - dy) % Y, (x - dx) % X, me]
        send(group, group, gs_s.at[g, j], gs_r.at[g, j], sib)

    def gather_z(g):
        for d in range(1, Z):
            block = held(g, d)
            arrived(block, gz_s.at[g, d - 1], gz_r.at[g, d - 1])
            for j, peer in enumerate(xy_peers):
                send(block, block, gx_s.at[g, d, j], gx_r.at[g, d, j], peer)
        to_sibling(g, 0)

    def gather_xy(g):
        packed(g, 0, me)
        for j, (dy, dx) in enumerate(offsets):
            for d in range(Z):
                block = full.at[g, (y - dy) % Y, (x - dx) % X, me, (z - d) % Z]
                arrived(block, gx_s.at[g, d, j], gx_r.at[g, d, j])
            to_sibling(g, j + 1)
            packed(g, j + 1, me)

    def packed(g, j, core):
        dy, dx = ([(0, 0)] + offsets)[j]
        yy, xx = (y - dy) % Y, (x - dx) % X
        size = 2 * Z * count
        place = stage.at[pl.ds(pl.multiple_of((yy * X + xx) * size, 8), size)]
        for zz in range(Z):
            for c in (0, 1):

                @pl.when(core == c)
                def _():
                    place[pl.ds((2 * zz + c) * count, count), :] = full[g, yy, xx, c, zz].astype(
                        jnp.float32
                    )

    def sources(g):
        for j, (dy, dx) in enumerate([(0, 0)] + offsets):
            group = full.at[g, (y - dy) % Y, (x - dx) % X, 1 - me]
            arrived(group, gs_s.at[g, j], gs_r.at[g, j])
            packed(g, j, 1 - me)
        data[...] = stage[...].astype(jnp.bfloat16)
        source = jnp.dot(operator[...], data[...], preferred_element_type=jnp.float32)
        tile = source.reshape(rows, cols, LANES) * inverse[...]
        s[g, pl.ds(m, rows), pl.ds(m, cols)] = tile
        top = top_of(tile, (0, 1))
        q_out[g] = coded(tile, top)
        q_scale[g] = jnp.broadcast_to(top[0] * (1.0 / LEVELS), (8, LANES))

    def halo_send(g):
        for i, (d, at) in enumerate(((north, 0), (south, rows - m))):
            has = exists(*d)
            send_if(
                has, q_out.at[g, pl.ds(at, m)], q_in.at[g, i], hq_s.at[g, i], hq_r.at[g, i],
                peer_of(d),
            )
            send_if(
                has, q_scale.at[g], q_in_scale.at[g, i], hc_s.at[g, i], hc_r.at[g, i], peer_of(d)
            )
        inner = pl.ds(m, rows)
        for i, (d, src, dst) in enumerate(((west, m, m + cols), (east, cols, 0))):
            send_if(
                exists(*d), s.at[g, inner, pl.ds(src, m)], s.at[g, inner, pl.ds(dst, m)],
                he_s.at[g, i], he_r.at[g, i], peer_of(d),
            )

    def halo_recv(g):
        for i, (d, at) in enumerate(((south, m + rows), (north, 0))):

            @pl.when(exists(*d))
            def _():
                arrived(q_in.at[g, i], hq_s.at[g, i], hq_r.at[g, i])
                arrived(q_in_scale.at[g, i], hc_s.at[g, i], hc_r.at[g, i])
                s[g, pl.ds(at, m), pl.ds(m, cols)] = decoded(
                    q_in[g, i], q_in_scale[g, i][:1][None]
                )

        for i, (d, src, dst) in enumerate(((west, m, m + cols), (east, cols, 0))):
            for k, at in enumerate((0, m + rows)):
                send_if(
                    exists(*d), s.at[g, pl.ds(at, m), pl.ds(src, m)],
                    s.at[g, pl.ds(at, m), pl.ds(dst, m)],
                    hk_s.at[g, i, k], hk_r.at[g, i, k], peer_of(d),
                )

    def halo_sides(g):
        for i, (d, dst) in enumerate(((east, m + cols), (west, 0))):

            @pl.when(exists(*d))
            def _():
                block = s.at[g, pl.ds(m, rows), pl.ds(dst, m)]
                arrived(block, he_s.at[g, i], he_r.at[g, i])
                for k, at in enumerate((0, m + rows)):
                    block = s.at[g, pl.ds(at, m), pl.ds(dst, m)]
                    arrived(block, hk_s.at[g, i, k], hk_r.at[g, i, k])

    def sweeps(g, hooks):
        turns = [u, v]
        fixed = s.at[g]
        for step in range(1, m + 1):
            if step in hooks:
                hooks[step]()
            old = fixed if step == 1 else turns[step % 2]
            new = turns[(step + 1) % 2]
            last = step == m

            def swept(r):
                centre = old[r]
                value = fixed[r] + coef[0, r] * old[r - 1]
                value = value + coef[1, r] * old[r + 1]
                value = value + coef[2, r] * pltpu.roll(centre, 1, 0)
                value = value + coef[3, r] * pltpu.roll(centre, wide_cols - 1, 0)
                if last:
                    done = value[m : m + cols]
                    prior[r - m, :, lanes(g)] = done
                    at = pl.multiple_of((r - m) * cols, cols)
                    smooth[pl.ds(at, cols), lanes(g)] = done.astype(jnp.bfloat16)
                else:
                    new[r] = value

            @pl.loop(0, (wide_rows - 2 * step) // 2)
            def _(i):
                swept(step + 2 * i)
                swept(step + 2 * i + 1)

    mine_rows = pl.ds(pl.multiple_of(me * start_row, 8), H)
    other_rows = pl.ds(pl.multiple_of((1 - me) * start_row, 8), H)
    groups = [*offsets, (0, 0)]

    def group_at(j):
        dy, dx = groups[j]
        return ((y + dy) % Y) * X + (x + dx) % X

    def forward(first, end):
        partial = lax.dot_general(
            operator[...], smooth[:, first * LANES : end * LANES], (((0,), (0,)), ((), ())),
            preferred_element_type=jnp.float32,
        )
        for g in range(first, end):
            part = partial[:, (g - first) * LANES : (g - first + 1) * LANES]
            if pair % 8 == 0:
                wide[g] = part.reshape(Y * X, Z, pair, LANES)
            else:
                flat[...] = part
                for k in range(chips):
                    wide[g, k // Z, k % Z, pl.ds(0, pair)] = flat[pl.ds(k * pair, pair)]
                    rest = wide.shape[3] - pair
                    wide[g, k // Z, k % Z, pl.ds(pair, rest)] = jnp.zeros(
                        (rest, LANES), jnp.float32
                    )
            for j in range(len(groups)):
                k = group_at(j)
                send(
                    wide.at[g, k, :, other_rows], sib_in.at[g, k], rs_s.at[g, j], rs_r.at[g, j],
                    sib,
                )

    def pair_sum(g, j, zz):
        k = group_at(j)
        return wide[g, k, zz, mine_rows] + sib_in[g, k, zz]

    turn = [*range(1, Z), 0]

    def scatter_xy(g):
        for j, peer in enumerate(xy_peers):
            k = group_at(j)
            arrived(sib_in.at[g, k], rs_s.at[g, j], rs_r.at[g, j])
            for d in range(Z):
                value = pair_sum(g, j, (z + turn[d]) % Z)
                top = top_of(value, (0,))
                xy_q[g, j, d] = coded(value, top)
                xy_c[g, j, pl.ds(d, 1)] = top * (1.0 / LEVELS)
            send(xy_c.at[g, j], xy_f.at[g, j], rc_s.at[g, j], rc_r.at[g, j], peer)
        for d in range(Z):
            for j, peer in enumerate(xy_peers):
                send(
                    xy_q.at[g, j, d], xy_r.at[g, j, d], rq_s.at[g, j, d], rq_r.at[g, j, d], peer
                )

    def scatter_z(g):
        j = len(xy_peers)
        arrived(sib_in.at[g, group_at(j)], rs_s.at[g, j], rs_r.at[g, j])
        for i in range(j):
            arrived(xy_f.at[g, i], rc_s.at[g, i], rc_r.at[g, i])
        for d in range(Z):
            value = pair_sum(g, j, (z + turn[d]) % Z)
            for i in range(j):
                arrived(xy_r.at[g, i, d], rq_s.at[g, i, d], rq_r.at[g, i, d])
                value = value + decoded(xy_r[g, i, d], xy_f[g, i, pl.ds(d, 1)])
            if d == Z - 1:
                own[g] = value
                break
            top = top_of(value, (0,))
            z_q[g, d] = coded(value, top)
            z_c[g, d] = jnp.broadcast_to(top * (1.0 / LEVELS), (8, LANES))
            send(z_c.at[g, d], z_f.at[g, d], zc_s.at[g, d], zc_r.at[g, d], z_peers[d])
            send(z_q.at[g, d], z_r.at[g, d], zq_s.at[g, d], zq_r.at[g, d], z_peers[d])

    def scatter_end(g):
        value = own[g]
        for d in range(1, Z):
            arrived(z_r.at[g, d - 1], zq_s.at[g, d - 1], zq_r.at[g, d - 1])
            arrived(z_f.at[g, d - 1], zc_s.at[g, d - 1], zc_r.at[g, d - 1])
            value = value + decoded(z_r[g, d - 1], z_f[g, d - 1][:1])
        out[:, lanes(g)] = value

    class_sides()
    for g in range(chunks):
        gather_z(g)
        if g == 0:
            coefficients()
    load.wait()
    for g in range(chunks):
        gather_xy(g)
        if g == chunks - 1 and g:
            halo_recv(0)
        sources(g)
        halo_send(g)
    if chunks == 1:
        halo_recv(0)
    waiting = []
    for g in range(chunks):
        halo_sides(g)
        hooks = {}
        if g + 1 < chunks:
            hooks[m // 2 + 1] = functools.partial(halo_recv, g + 1)
        for step, k in zip((m // 2 - 1, m - 1), waiting):
            hooks[step] = functools.partial(scatter_xy, k)
        sweeps(g, hooks)
        sent, waiting = waiting, []
        for k in sent[:1]:
            scatter_z(k)
        if g % 2 or g == chunks - 1:
            first = g - g % 2
            forward(first, g + 1)
            waiting = [*range(first, g + 1)]
        for k in sent[1:]:
            scatter_z(k)
    for k in waiting:
        scatter_xy(k)
    for k in range(waiting[0]):
        scatter_end(k)
    for k in waiting:
        scatter_z(k)
    for k in waiting:
        scatter_end(k)
    for has, copy in pending:
        if has is None:
            copy.wait_send()
        else:

            @pl.when(has)
            def _():
                copy.wait_send()


def local(operator_t, data_columns, noise_var, class_map, diffusion_table, kappa_table):
    rows, cols, data_rows = operator_t.shape
    count, width = data_columns.shape
    gx_size, gy_size = lax.axis_size("gx"), lax.axis_size("gy")
    X = 2
    Y, Z = gx_size // X, gy_size // 2
    chips = Y * X * Z
    points = rows * cols
    chunks = width // LANES
    m = ITERS
    start = count // 8 * 8
    H = max(up8(count), up8(2 * count) - start)
    tall = max(start + H, 2 * count)
    f32, bf16, i16, i32 = jnp.float32, jnp.bfloat16, jnp.int16, jnp.int32
    peers, zs = Y * X - 1, max(Z - 1, 1)

    def vmem(*shape, kind=f32):
        return pltpu.VMEM(shape, kind)

    def sems(*shape):
        return [pltpu.SemaphoreType.DMA(shape)] * 2

    field = (rows + 2 * m, cols + 2 * m)
    even = 2 * count % 8 == 0
    scratch = [
        vmem(points, data_rows, kind=bf16),
        vmem(3, rows, LANES, kind=i32),
        vmem(chunks, Y, X, 2, Z, count, LANES, kind=bf16),
        vmem(data_rows, LANES),
        vmem(data_rows, LANES, kind=bf16),
        vmem(2, 3, rows, LANES, kind=i32),
        vmem(4, *field, LANES),
        vmem(rows, cols, LANES),
        vmem(chunks, *field, LANES),
        vmem(*field, LANES),
        vmem(*field, LANES),
        vmem(chunks, rows, cols, LANES, kind=i16),
        vmem(chunks, 8, LANES),
        vmem(chunks, 2, m, cols, LANES, kind=i16),
        vmem(chunks, 2, 8, LANES),
        vmem(points, width, kind=bf16),
        vmem(*((8,) if even else (data_rows,)), LANES),
        vmem(chunks, Y * X, Z, tall, LANES),
        vmem(chunks, Y * X, Z, H, LANES),
        vmem(chunks, peers, Z, H, LANES, kind=i16),
        vmem(chunks, peers, Z, LANES),
        vmem(chunks, peers, Z, H, LANES, kind=i16),
        vmem(chunks, peers, Z, LANES),
        vmem(chunks, zs, H, LANES, kind=i16),
        vmem(chunks, zs, 8, LANES),
        vmem(chunks, zs, H, LANES, kind=i16),
        vmem(chunks, zs, 8, LANES),
        vmem(chunks, H, LANES),
        pltpu.SemaphoreType.DMA,
        pltpu.SemaphoreType.DMA((chunks,)),
        *sems(4),
        *sems(chunks, zs),
        *sems(chunks, Z, peers),
        *sems(chunks, peers + 1),
        *sems(chunks, 2),
        *sems(chunks, 2),
        *sems(chunks, 2),
        *sems(chunks, 2, 2),
        *sems(chunks, peers + 1),
        *sems(chunks, peers, Z),
        *sems(chunks, peers),
        *sems(chunks, zs),
        *sems(chunks, zs),
    ]
    block = pl.BlockSpec(memory_space=pltpu.VMEM)
    table = pl.BlockSpec(memory_space=pltpu.SMEM)
    anywhere = pl.BlockSpec(memory_space=pl.ANY)
    out, prior = pl.pallas_call(
        functools.partial(block_kernel, (Y, X, Z), (gx_size, gy_size), start, H),
        out_shape=(
            jax.ShapeDtypeStruct((H, width), f32),
            jax.ShapeDtypeStruct((rows, cols, width), f32),
        ),
        in_specs=[anywhere, block, table, table, anywhere],
        out_specs=(block, block),
        scratch_shapes=scratch,
        compiler_params=pltpu.CompilerParams(
            collective_id=0, has_side_effects=True, vmem_limit_bytes=52 << 20
        ),
    )(data_columns, class_map, diffusion_table, kappa_table, operator_t.reshape(points, data_rows))
    core = lax.axis_index("gy") % 2
    forward = jnp.where(core == 0, out[:count], out[count - start : 2 * count - start])
    return (forward + noise_var[:, None] * data_columns.astype(f32), prior)


def solution(mesh):
    placed = (P("gx", "gy", None), P(("gx", "gy"), None), P(("gx", "gy")), P("gx", "gy"), P(), P())
    return jax.shard_map(
        local,
        mesh=mesh,
        in_specs=placed,
        out_specs=(P(("gx", "gy"), None), P("gx", "gy", None)),
        check_vma=False,
    )
```

time: 77.6 us -> 72.7 us (0.937)
  Pallas kernels: 70.9 us -> 67.1 us
  other arithmetic: 1.71 us -> 0.73 us
    pallas_call x1, Pallas kernels: 70.9 us -> 67.1 us  [local(): pl.pallas_call(functools.partial(block_kernel, (Y, X, Z), (gx_size, gy_si...]
    pad x1 -> x0, local copies, waits for them, and re-layouts: 1.3 us -> none  [local(): jnp.pad(class_map, ((0, 0), (0, LANES - cols)), constant_values=-1)]
    unnamed x5 -> x11, local copies, waits for them, and re-layouts: 2.71 us -> 3.97 us
    add x1, other arithmetic: 1.71 us -> 0.73 us  [local(): return (forward + noise_var[:, None] * data_columns.astype(f32), prior)]
where the time goes in v1:
time: 72.7 us; the launch traced here: 72.4 us
  Pallas kernels  67.1 us (92%)
  local copies, waits for them, and re-layouts  3.97 us (5%)
  other arithmetic  0.73 us (1%)
    pallas_call x1, Pallas kernels, local(): pl.pallas_call(functools.partial(block_kernel, (Y, X, Z), (gx_size, gy_si...  67.1 us
    unnamed x11, local copies, waits for them, and re-layouts  3.97 us

profile of v1, /device:TPU:0, one launch (start us, length us, event | category | flops | bytes accessed | tf_op | source)
XLA Modules:
  0.0 72.4 jit_solution(3011812979710014168)
XLA Ops:
  0.6 0.0 copy-start
  0.7 0.8 %copy-done = bf16[76,384]{1,0:T(8,128)(2,1)S(1)} copy-done((bf16[76,384]{1,0:T(8,128)(2,1)S(1)}, bf16[76,384]{1,0:T(8,128)(2,1)}, u32[]{:S(2)}) %copy-start) | copy-done | bytes 58392
  1.5 0.0 copy-start.1
  1.5 0.7 copy-done.1
  2.2 0.0 copy-start.2
  2.2 0.7 copy-done.2
  2.8 0.0 copy-start.3
  2.8 0.7 copy-done.3
  3.5 0.0 copy-start.4
  3.5 67.1 %shard_map.77 = (f32[80,384]{1,0:T(8,128)S(1)}, f32[16,64,384]{2,1,0:T(8,128)S(1)}) custom-call(bf16[76,384]{1,0:T(8,128)(2,1)S(1)} %copy-done, s32[16,64]{1,0:T(8,128)S(1)} %copy-done.1, f32[16]{0:T(128)S(1)} %copy-done.2, f32[16]{0:T(128)S(1)} %copy-done.3, bf16[1024,2432]{1,0:T(8,128)(2,1)} %bitcast.1), custom_call_target="tpu_custom_call" | custom-call | tf_op jit(solution)/shard_map/pallas_call | solution.py:556
  70.5 0.0 copy-done.4
  70.6 0.7 %multiply_add_fusion = f32[76,384]{1,0:T(8,128)} fusion(bf16[76,384]{1,0:T(8,128)(2,1)S(1)} %copy-done, f32[80,384]{1,0:T(8,128)S(1)} %get-tuple-element.4, f32[76]{0:T(128)S(1)} %copy-done.4, pred[]{:T(512)S(6)} %eq.5), kind=kLoop, calls=%fused_computation | loop fusion | flops 116736 | bytes 408881 | tf_op jit(solution)/shard_map/add | solution.py:571
  71.3 1.1 %copy.9 = f32[16,64,384]{2,1,0:T(8,128)} copy(f32[16,64,384]{2,1,0:T(8,128)S(1)} %get-tuple-element.9) | data formatting | bytes 3145728
Async XLA Ops:
  0.6 0.8 %copy-start = (bf16[76,384]{1,0:T(8,128)(2,1)S(1)}, bf16[76,384]{1,0:T(8,128)(2,1)}, u32[]{:S(2)}) copy-start(bf16[76,384]{1,0:T(8,128)(2,1)} %mine.1) | copy-start | bytes 175108
  1.5 0.7 copy-start.1
  2.2 0.7 copy-start.2
  2.8 0.7 copy-start.3
  3.5 67.1 %copy-start.4 = (f32[76]{0:T(128)S(1)}, f32[76]{0:T(128)}, u32[]{:S(2)}) copy-start(f32[76]{0:T(128)} %param.8) | copy-start | bytes 916

commit v2 on v1

--- a/solution.py
+++ b/solution.py
@@ -36,19 +36,19 @@
 
 def block_kernel(
     dims, counts, start_row, H,
-    mine, class_map, diffusion_table, kappa_table, operator_hbm,
-    out, prior,
-    operator, classes, full, stage, data, near_classes, coef, inverse,
+    mine, class_map, diffusion_hbm, kappa_hbm, operator_hbm,
+    out_hbm, prior_hbm,
+    out, prior, class_in, diffusion_table, kappa_table, operator, classes, thin, full, stage, data, near_classes, coef, inverse,
     s, u, v, q_out, q_scale, q_in, q_in_scale, smooth,
     flat, wide, sib_in, xy_q, xy_c, xy_r, xy_f, z_q, z_c, z_r, z_f, own,
-    op_sem, own_sem, cls_s, cls_r, gz_s, gz_r, gx_s, gx_r, gs_s, gs_r,
+    op_sem, in_sem, out_sem, own_sem, cls_s, cls_r, gz_s, gz_r, gx_s, gx_r, gs_s, gs_r,
     hq_s, hq_r, hc_s, hc_r, he_s, he_r, hk_s, hk_r,
     rs_s, rs_r, rq_s, rq_r, rc_s, rc_r, zq_s, zq_r, zc_s, zc_r,
 ):
     Y, X, Z = dims
     m = ITERS
     chunks = s.shape[0]
-    rows, cols = prior.shape[0], prior.shape[1]
+    rows, cols = prior.shape[1], prior.shape[2]
     count = mine.shape[0]
     pair = 2 * count
     chips = Y * X * Z
@@ -75,7 +75,7 @@
     def lanes(g):
         return pl.ds(g * LANES, LANES)
 
-    pending = []
+    pending, results = [], []
 
     def send(src, dst, sends, recvs, peer):
         copy = remote(src, dst, sends, recvs, peer)
@@ -102,8 +102,14 @@
     ]
     for copy in homes:
         copy.start()
+    small = [
+        pltpu.make_async_copy(class_map, class_in, in_sem.at[0]),
+        pltpu.make_async_copy(diffusion_hbm, diffusion_table, in_sem.at[1]),
+        pltpu.make_async_copy(kappa_hbm, kappa_table, in_sem.at[2]),
+    ]
+    for copy in small:
+        copy.start()
     classes[...] = jnp.full(classes.shape, -1, jnp.int32)
-    classes[1, :, pl.ds(0, cols)] = class_map[...]
 
     wide_rows, wide_cols = rows + 2 * m, cols + 2 * m
     for (dr, dc), where in (
@@ -120,6 +126,9 @@
                     (where[0].size, where[1].size, LANES), jnp.float32
                 )
 
+    for copy in small:
+        copy.wait()
+    classes[1, :, pl.ds(0, cols)] = class_in[...]
     ready = pltpu.get_barrier_semaphore()
     for peer in [sib, *z_peers, *xy_peers]:
         pl.semaphore_signal(ready, inc=1, device_id=peer, device_id_type=MESH)
@@ -214,13 +223,16 @@
             return padded.T
 
         for i, w in enumerate(weights):
-            turned = upright(jnp.where(inside, w / divisor, 0.0))
-            for r in range(wide_rows):
-                coef[i, r] = jnp.broadcast_to(turned[:wide_cols, r : r + 1], (wide_cols, LANES))
+            thin[i] = upright(jnp.where(inside, w / divisor, 0.0))
         turned = upright(1.0 / divisor)
         for r in range(rows):
             inverse[r] = jnp.broadcast_to(turned[m : m + cols, m + r : m + r + 1], (cols, LANES))
 
+
+    def coefficient(i):
+        turned = thin[i]
+        for r in range(wide_rows):
+            coef[i, r] = jnp.broadcast_to(turned[:wide_cols, r : r + 1], (wide_cols, LANES))
 
     def held(g, d, core=me):
         return full.at[g, y, x, core, (z - d) % Z]
@@ -261,18 +273,31 @@
                         jnp.float32
                     )
 
-    def sources(g):
+    def sib_blocks(g):
         for j, (dy, dx) in enumerate([(0, 0)] + offsets):
             group = full.at[g, (y - dy) % Y, (x - dx) % X, 1 - me]
             arrived(group, gs_s.at[g, j], gs_r.at[g, j])
             packed(g, j, 1 - me)
-        data[...] = stage[...].astype(jnp.bfloat16)
-        source = jnp.dot(operator[...], data[...], preferred_element_type=jnp.float32)
-        tile = source.reshape(rows, cols, LANES) * inverse[...]
-        s[g, pl.ds(m, rows), pl.ds(m, cols)] = tile
-        top = top_of(tile, (0, 1))
-        q_out[g] = coded(tile, top)
-        q_scale[g] = jnp.broadcast_to(top[0] * (1.0 / LEVELS), (8, LANES))
+        data[:, lanes(g)] = stage[...].astype(jnp.bfloat16)
+
+    def sources(first, end):
+        half = operator.shape[0] // 2
+        right = data[:, first * LANES : end * LANES]
+        source = jnp.concatenate(
+            [
+                jnp.dot(operator[rows_of, :], right, preferred_element_type=jnp.float32)
+                for rows_of in (pl.ds(0, half), pl.ds(half, half))
+            ],
+            axis=0,
+        )
+        for g in range(first, end):
+            part = source[:, (g - first) * LANES : (g - first + 1) * LANES]
+            tile = part.reshape(rows, cols, LANES) * inverse[...]
+            s[g, pl.ds(m, rows), pl.ds(m, cols)] = tile
+            top = top_of(tile, (0, 1))
+            q_out[g] = coded(tile, top)
+            q_scale[g] = jnp.broadcast_to(top[0] * (1.0 / LEVELS), (8, LANES))
+            halo_send(g)
 
     def halo_send(g):
         for i, (d, at) in enumerate(((north, 0), (south, rows - m))):
@@ -339,7 +364,7 @@
                 value = value + coef[3, r] * pltpu.roll(centre, wide_cols - 1, 0)
                 if last:
                     done = value[m : m + cols]
-                    prior[r - m, :, lanes(g)] = done
+                    prior[g, r - m] = done
                     at = pl.multiple_of((r - m) * cols, cols)
                     smooth[pl.ds(at, cols), lanes(g)] = done.astype(jnp.bfloat16)
                 else:
@@ -350,6 +375,11 @@
                 swept(step + 2 * i)
                 swept(step + 2 * i + 1)
 
+        results.append(
+            pltpu.make_async_copy(prior.at[g], prior_hbm.at[:, :, lanes(g)], out_sem.at[1, g])
+        )
+        results[-1].start()
+
     mine_rows = pl.ds(pl.multiple_of(me * start_row, 8), H)
     other_rows = pl.ds(pl.multiple_of((1 - me) * start_row, 8), H)
     groups = [*offsets, (0, 0)]
@@ -359,9 +389,18 @@
         return ((y + dy) % Y) * X + (x + dx) % X
 
     def forward(first, end):
-        partial = lax.dot_general(
-            operator[...], smooth[:, first * LANES : end * LANES], (((0,), (0,)), ((), ())),
-            preferred_element_type=jnp.float32,
+        total_rows = operator.shape[1]
+        cut = -(-total_rows // 2 // LANES) * LANES
+        right = smooth[:, first * LANES : end * LANES]
+        partial = jnp.concatenate(
+            [
+                lax.dot_general(
+                    operator[:, part], right, (((0,), (0,)), ((), ())),
+                    preferred_element_type=jnp.float32,
+                )
+                for part in (pl.ds(0, cut), pl.ds(cut, total_rows - cut))
+            ],
+            axis=0,
         )
         for g in range(first, end):
             part = partial[:, (g - first) * LANES : (g - first + 1) * LANES]
@@ -429,48 +468,46 @@
             arrived(z_r.at[g, d - 1], zq_s.at[g, d - 1], zq_r.at[g, d - 1])
             arrived(z_f.at[g, d - 1], zc_s.at[g, d - 1], zc_r.at[g, d - 1])
             value = value + decoded(z_r[g, d - 1], z_f[g, d - 1][:1])
-        out[:, lanes(g)] = value
+        out[g] = value
+        results.append(pltpu.make_async_copy(out.at[g], out_hbm.at[:, lanes(g)], out_sem.at[0, g]))
+        results[-1].start()
 
     class_sides()
     for g in range(chunks):
         gather_z(g)
         if g == 0:
             coefficients()
+        else:
+            coefficient(g - 1)
+    for i in range(chunks - 1, 4):
+        coefficient(i)
     load.wait()
-    for g in range(chunks):
+    gather_xy(0)
+    sib_blocks(0)
+    sources(0, 1)
+    for g in range(1, chunks):
         gather_xy(g)
-        if g == chunks - 1 and g:
-            halo_recv(0)
-        sources(g)
-        halo_send(g)
-    if chunks == 1:
-        halo_recv(0)
-    waiting = []
+        sib_blocks(g)
+        sources(g, g + 1)
+    halo_recv(0)
     for g in range(chunks):
         halo_sides(g)
-        hooks = {}
+        sweeps(g, {2: functools.partial(scatter_xy, g - 1)} if g else {})
         if g + 1 < chunks:
-            hooks[m // 2 + 1] = functools.partial(halo_recv, g + 1)
-        for step, k in zip((m // 2 - 1, m - 1), waiting):
-            hooks[step] = functools.partial(scatter_xy, k)
-        sweeps(g, hooks)
-        sent, waiting = waiting, []
-        for k in sent[:1]:
-            scatter_z(k)
-        if g % 2 or g == chunks - 1:
-            first = g - g % 2
-            forward(first, g + 1)
-            waiting = [*range(first, g + 1)]
-        for k in sent[1:]:
-            scatter_z(k)
-    for k in waiting:
-        scatter_xy(k)
-    for k in range(waiting[0]):
-        scatter_end(k)
-    for k in waiting:
-        scatter_z(k)
-    for k in waiting:
-        scatter_end(k)
+            halo_recv(g + 1)
+        forward(g, g + 1)
+    last = chunks - 1
+    for g in range(last - 1):
+        scatter_z(g)
+    scatter_xy(last)
+    for g in range(max(last - 1, 0), last):
+        scatter_z(g)
+    for g in range(last):
+        scatter_end(g)
+    scatter_z(last)
+    scatter_end(last)
+    for copy in results:
+        copy.wait()
     for has, copy in pending:
         if has is None:
             copy.wait_send()
@@ -506,11 +543,17 @@
     field = (rows + 2 * m, cols + 2 * m)
     even = 2 * count % 8 == 0
     scratch = [
+        vmem(chunks, H, LANES),
+        vmem(chunks, rows, cols, LANES),
+        vmem(rows, cols, kind=i32),
+        pltpu.SMEM(diffusion_table.shape, f32),
+        pltpu.SMEM(kappa_table.shape, f32),
         vmem(points, data_rows, kind=bf16),
         vmem(3, rows, LANES, kind=i32),
+        vmem(4, LANES, LANES),
         vmem(chunks, Y, X, 2, Z, count, LANES, kind=bf16),
         vmem(data_rows, LANES),
-        vmem(data_rows, LANES, kind=bf16),
+        vmem(data_rows, width, kind=bf16),
         vmem(2, 3, rows, LANES, kind=i32),
         vmem(4, *field, LANES),
         vmem(rows, cols, LANES),
@@ -535,6 +578,8 @@
         vmem(chunks, zs, 8, LANES),
         vmem(chunks, H, LANES),
         pltpu.SemaphoreType.DMA,
+        pltpu.SemaphoreType.DMA((3,)),
+        pltpu.SemaphoreType.DMA((2, chunks)),
         pltpu.SemaphoreType.DMA((chunks,)),
         *sems(4),
         *sems(chunks, zs),
@@ -550,22 +595,21 @@
         *sems(chunks, zs),
         *sems(chunks, zs),
     ]
-    block = pl.BlockSpec(memory_space=pltpu.VMEM)
-    table = pl.BlockSpec(memory_space=pltpu.SMEM)
     anywhere = pl.BlockSpec(memory_space=pl.ANY)
+    hbm = pl.BlockSpec(memory_space=pltpu.HBM)
     out, prior = pl.pallas_call(
         functools.partial(block_kernel, (Y, X, Z), (gx_size, gy_size), start, H),
         out_shape=(
             jax.ShapeDtypeStruct((H, width), f32),
             jax.ShapeDtypeStruct((rows, cols, width), f32),
         ),
-        in_specs=[anywhere, block, table, table, anywhere],
-        out_specs=(block, block),
+        in_specs=[hbm] * 5,
+        out_specs=(anywhere, anywhere),
         scratch_shapes=scratch,
         compiler_params=pltpu.CompilerParams(
             collective_id=0, has_side_effects=True, vmem_limit_bytes=52 << 20
         ),
-    )(data_columns, class_map, diffusion_table, kappa_table, operator_t.reshape(points, data_rows))
+    )(*[pltpu.with_memory_space_constraint(a, pltpu.HBM) for a in (data_columns, class_map, diffusion_table, kappa_table, operator_t.reshape(points, data_rows))])
     core = lax.axis_index("gy") % 2
     forward = jnp.where(core == 0, out[:count], out[count - start : 2 * count - start])
     return (forward + noise_var[:, None] * data_columns.astype(f32), prior)

time: 72.7 us -> 63.5 us (0.87)
  Pallas kernels: 67.1 us -> 60.8 us
  local copies, waits for them, and re-layouts: 3.97 us -> 1.15 us
    pallas_call x1, Pallas kernels: 67.1 us -> 60.8 us  [local(): pl.pallas_call(functools.partial(block_kernel, (Y, X, Z), (gx_size, gy_si...]
    unnamed x11 -> x5, local copies, waits for them, and re-layouts: 3.97 us -> 1.15 us
where the time goes in v2:
time: 63.5 us; the launch traced here: 63.4 us
  Pallas kernels  60.8 us (96%)
  local copies, waits for them, and re-layouts  1.15 us (2%)
  other arithmetic  0.73 us (1%)
  between operations  0.69 us (1%)
    pallas_call x1, Pallas kernels, local(): pl.pallas_call(functools.partial(block_kernel, (Y, X, Z), (gx_size, gy_si...  60.8 us

profile of v2, /device:TPU:0, one launch (start us, length us, event | category | flops | bytes accessed | tf_op | source)
XLA Modules:
  0.0 63.4 jit_solution(11669301058153550326)
XLA Ops:
  0.6 0.0 copy-start
  0.7 0.0 copy-start.1
  0.7 60.8 %shard_map.77 = (f32[80,384]{1,0:T(8,128)S(1)}, f32[16,64,384]{2,1,0:T(8,128)S(1)}) custom-call(bf16[76,384]{1,0:T(8,128)(2,1)} %mine.1, s32[16,64]{1,0:T(8,128)} %class_map.1, f32[16]{0:T(128)} %diffusion_hbm.1, f32[16]{0:T(128)} %kappa_hbm.1, bf16[1024,2432]{1,0:T(8,128)(2,1)} %bitcast.1), custom_call_target="tpu_custom_call" | custom-call | tf_op jit(solution)/shard_map/pallas_call | solution.py:600
  61.5 0.0 copy-done
  61.5 0.0 copy-done.1
  61.5 0.7 %multiply_add_fusion = f32[76,384]{1,0:T(8,128)} fusion(bf16[76,384]{1,0:T(8,128)(2,1)S(1)} %copy-done, f32[80,384]{1,0:T(8,128)S(1)} %get-tuple-element.4, f32[76]{0:T(128)S(1)} %copy-done.1, pred[]{:T(512)S(6)} %eq.5), kind=kLoop, calls=%fused_computation | loop fusion | flops 116736 | bytes 408881 | tf_op jit(solution)/shard_map/add | solution.py:615
  62.2 1.1 %copy.9 = f32[16,64,384]{2,1,0:T(8,128)} copy(f32[16,64,384]{2,1,0:T(8,128)S(1)} %get-tuple-element.9) | data formatting | bytes 3145728
Async XLA Ops:
  0.6 60.8 %copy-start = (bf16[76,384]{1,0:T(8,128)(2,1)S(1)}, bf16[76,384]{1,0:T(8,128)(2,1)}, u32[]{:S(2)}) copy-start(bf16[76,384]{1,0:T(8,128)(2,1)} %mine.1) | copy-start | bytes 175108
  0.7 60.8 %copy-start.1 = (f32[76]{0:T(128)S(1)}, f32[76]{0:T(128)}, u32[]{:S(2)}) copy-start(f32[76]{0:T(128)} %param.8) | copy-start | bytes 916

commit v3 on v2

--- a/solution.py
+++ b/solution.py
@@ -42,7 +42,7 @@
     s, u, v, q_out, q_scale, q_in, q_in_scale, smooth,
     flat, wide, sib_in, xy_q, xy_c, xy_r, xy_f, z_q, z_c, z_r, z_f, own,
     op_sem, in_sem, out_sem, own_sem, cls_s, cls_r, gz_s, gz_r, gx_s, gx_r, gs_s, gs_r,
-    hq_s, hq_r, hc_s, hc_r, he_s, he_r, hk_s, hk_r,
+    hq_s, hq_r, hc_s, hc_r, he_s, he_r,
     rs_s, rs_r, rq_s, rq_r, rc_s, rc_r, zq_s, zq_r, zc_s, zc_r,
 ):
     Y, X, Z = dims
@@ -75,29 +75,27 @@
     def lanes(g):
         return pl.ds(g * LANES, LANES)
 
-    pending, results = [], []
-
-    def send(src, dst, sends, recvs, peer):
-        copy = remote(src, dst, sends, recvs, peer)
-        copy.start()
-        pending.append((None, copy))
-
-    def send_if(has, src, dst, sends, recvs, peer):
-        copy = remote(src, dst, sends, recvs, peer)
-
-        @pl.when(has)
-        def _():
-            copy.start()
-
-        pending.append((has, copy))
-
-    def arrived(ref, sends, recvs):
-        remote(ref, ref, sends, recvs, sib).wait_recv()
+    pending = []
+
+    def send(src, dst, sends, recvs, peer, has=None):
+        if has is None:
+            remote(src, dst, sends, recvs, peer).start()
+        else:
+
+            @pl.when(has)
+            def _():
+                remote(src, dst, sends, recvs, peer).start()
+
+    def sent(ref, sends, has=None):
+        pending.append((has, remote(ref, ref, sends, sends, sib)))
+
+    def arrived(ref, recvs):
+        remote(ref, ref, recvs, recvs, sib).wait_recv()
 
     load = pltpu.make_async_copy(operator_hbm, operator, op_sem)
     load.start()
     homes = [
-        pltpu.make_async_copy(mine.at[:, lanes(g)], full.at[g, y, x, me, z], own_sem.at[g])
+        pltpu.make_async_copy(mine.at[:, lanes(g)], full.at[g, y, x, me, z], own_sem)
         for g in range(chunks)
     ]
     for copy in homes:
@@ -150,39 +148,42 @@
 
     def class_sides_send():
         for i, (d, slot) in enumerate(((west, 2), (east, 0))):
-            send_if(
-                exists(*d), classes.at[1], classes.at[slot], cls_s.at[i], cls_r.at[i], peer_of(d)
-            )
+            has = exists(*d)
+            send(classes.at[1], classes.at[slot], cls_s.at[i], cls_r.at[i], peer_of(d), has)
+            sent(classes.at[1], cls_s.at[i], has)
 
     def class_sides():
         for i, (d, slot) in enumerate(((east, 2), (west, 0))):
 
             @pl.when(exists(*d))
             def _():
-                arrived(classes.at[slot], cls_s.at[i], cls_r.at[i])
+                arrived(classes.at[slot], cls_r.at[i])
 
         for i, (d, slot) in enumerate(((north, 1), (south, 0))):
-            send_if(
-                exists(*d), classes, near_classes.at[slot], cls_s.at[2 + i], cls_r.at[2 + i],
-                peer_of(d),
-            )
+            has, at = exists(*d), 2 + i
+            send(classes, near_classes.at[slot], cls_s.at[at], cls_r.at[at], peer_of(d), has)
+            sent(classes, cls_s.at[at], has)
 
     class_sides_send()
-    for copy in homes:
-        copy.wait()
+    home = full.at[:, y, x, me, z]
+    pltpu.make_async_copy(home, home, own_sem).wait()
     for g in range(chunks):
         home = full.at[g, y, x, me, z]
         for d in range(1, Z):
-            send(home, home, gz_s.at[g, d - 1], gz_r.at[g, d - 1], z_peers[d - 1])
+            send(home, home, gz_s.at[g], gz_r.at[g, d - 1], z_peers[d - 1])
         for j, peer in enumerate(xy_peers):
-            send(home, home, gx_s.at[g, 0, j], gx_r.at[g, 0, j], peer)
+            send(home, home, gx_s.at[g, j], gx_r.at[g, j], peer)
+            sent(full.at[g, 0, 0, 0], gx_s.at[g, j])
+        if Z > 1:
+            sent(full.at[g, 0, 0, 0, pl.ds(0, Z - 1)], gz_s.at[g])
+        sent(full.at[g, :, :, 0], gs_s.at[g])
 
     def coefficients():
         for i, (d, slot) in enumerate(((south, 1), (north, 0))):
 
             @pl.when(exists(*d))
             def _():
-                arrived(near_classes.at[slot], cls_s.at[2 + i], cls_r.at[2 + i])
+                arrived(near_classes.at[slot], cls_r.at[2 + i])
 
             @pl.when(jnp.logical_not(exists(*d)))
             def _():
@@ -240,22 +241,20 @@
     def to_sibling(g, j):
         dy, dx = ([(0, 0)] + offsets)[j]
         group = full.at[g, (y - dy) % Y, (x - dx) % X, me]
-        send(group, group, gs_s.at[g, j], gs_r.at[g, j], sib)
+        send(group, group, gs_s.at[g], gs_r.at[g], sib)
 
     def gather_z(g):
         for d in range(1, Z):
             block = held(g, d)
-            arrived(block, gz_s.at[g, d - 1], gz_r.at[g, d - 1])
+            arrived(block, gz_r.at[g, d - 1])
             for j, peer in enumerate(xy_peers):
-                send(block, block, gx_s.at[g, d, j], gx_r.at[g, d, j], peer)
+                send(block, block, gx_s.at[g, j], gx_r.at[g, j], peer)
         to_sibling(g, 0)
 
     def gather_xy(g):
         packed(g, 0, me)
         for j, (dy, dx) in enumerate(offsets):
-            for d in range(Z):
-                block = full.at[g, (y - dy) % Y, (x - dx) % X, me, (z - d) % Z]
-                arrived(block, gx_s.at[g, d, j], gx_r.at[g, d, j])
+            arrived(full.at[g, (y - dy) % Y, (x - dx) % X, me], gx_r.at[g, j])
             to_sibling(g, j + 1)
             packed(g, j + 1, me)
 
@@ -274,9 +273,8 @@
                     )
 
     def sib_blocks(g):
-        for j, (dy, dx) in enumerate([(0, 0)] + offsets):
-            group = full.at[g, (y - dy) % Y, (x - dx) % X, 1 - me]
-            arrived(group, gs_s.at[g, j], gs_r.at[g, j])
+        arrived(full.at[g, :, :, 1 - me], gs_r.at[g])
+        for j in range(len(offsets) + 1):
             packed(g, j, 1 - me)
         data[:, lanes(g)] = stage[...].astype(jnp.bfloat16)
 
@@ -296,43 +294,41 @@
             s[g, pl.ds(m, rows), pl.ds(m, cols)] = tile
             top = top_of(tile, (0, 1))
             q_out[g] = coded(tile, top)
-            q_scale[g] = jnp.broadcast_to(top[0] * (1.0 / LEVELS), (8, LANES))
+            q_scale[g] = top[0] * (1.0 / LEVELS)
             halo_send(g)
+
+    strip = pl.ds(0, wide_rows)
 
     def halo_send(g):
         for i, (d, at) in enumerate(((north, 0), (south, rows - m))):
-            has = exists(*d)
-            send_if(
-                has, q_out.at[g, pl.ds(at, m)], q_in.at[g, i], hq_s.at[g, i], hq_r.at[g, i],
-                peer_of(d),
-            )
-            send_if(
-                has, q_scale.at[g], q_in_scale.at[g, i], hc_s.at[g, i], hc_r.at[g, i], peer_of(d)
-            )
+            has, peer = exists(*d), peer_of(d)
+            send(q_out.at[g, pl.ds(at, m)], q_in.at[g, i], hq_s.at[g, i], hq_r.at[g, i], peer, has)
+            send(q_scale.at[g], q_in_scale.at[g, i], hc_s.at[g, i], hc_r.at[g, i], peer, has)
+            sent(q_in.at[g, i], hq_s.at[g, i], has)
+            sent(q_scale.at[g], hc_s.at[g, i], has)
         inner = pl.ds(m, rows)
         for i, (d, src, dst) in enumerate(((west, m, m + cols), (east, cols, 0))):
-            send_if(
-                exists(*d), s.at[g, inner, pl.ds(src, m)], s.at[g, inner, pl.ds(dst, m)],
-                he_s.at[g, i], he_r.at[g, i], peer_of(d),
+            has = exists(*d)
+            send(
+                s.at[g, inner, pl.ds(src, m)], s.at[g, inner, pl.ds(dst, m)],
+                he_s.at[g, i], he_r.at[g, i], peer_of(d), has,
             )
+            sent(s.at[g, strip, pl.ds(src, m)], he_s.at[g, i], has)
 
     def halo_recv(g):
         for i, (d, at) in enumerate(((south, m + rows), (north, 0))):
 
             @pl.when(exists(*d))
             def _():
-                arrived(q_in.at[g, i], hq_s.at[g, i], hq_r.at[g, i])
-                arrived(q_in_scale.at[g, i], hc_s.at[g, i], hc_r.at[g, i])
-                s[g, pl.ds(at, m), pl.ds(m, cols)] = decoded(
-                    q_in[g, i], q_in_scale[g, i][:1][None]
-                )
+                arrived(q_in.at[g, i], hq_r.at[g, i])
+                arrived(q_in_scale.at[g, i], hc_r.at[g, i])
+                s[g, pl.ds(at, m), pl.ds(m, cols)] = decoded(q_in[g, i], q_in_scale[g, i][None])
 
         for i, (d, src, dst) in enumerate(((west, m, m + cols), (east, cols, 0))):
-            for k, at in enumerate((0, m + rows)):
-                send_if(
-                    exists(*d), s.at[g, pl.ds(at, m), pl.ds(src, m)],
-                    s.at[g, pl.ds(at, m), pl.ds(dst, m)],
-                    hk_s.at[g, i, k], hk_r.at[g, i, k], peer_of(d),
+            for at in (0, m + rows):
+                send(
+                    s.at[g, pl.ds(at, m), pl.ds(src, m)], s.at[g, pl.ds(at, m), pl.ds(dst, m)],
+                    he_s.at[g, i], he_r.at[g, i], peer_of(d), exists(*d),
                 )
 
     def halo_sides(g):
@@ -340,11 +336,7 @@
 
             @pl.when(exists(*d))
             def _():
-                block = s.at[g, pl.ds(m, rows), pl.ds(dst, m)]
-                arrived(block, he_s.at[g, i], he_r.at[g, i])
-                for k, at in enumerate((0, m + rows)):
-                    block = s.at[g, pl.ds(at, m), pl.ds(dst, m)]
-                    arrived(block, hk_s.at[g, i, k], hk_r.at[g, i, k])
+                arrived(s.at[g, strip, pl.ds(dst, m)], he_r.at[g, i])
 
     def sweeps(g, hooks):
         turns = [u, v]
@@ -375,10 +367,7 @@
                 swept(step + 2 * i)
                 swept(step + 2 * i + 1)
 
-        results.append(
-            pltpu.make_async_copy(prior.at[g], prior_hbm.at[:, :, lanes(g)], out_sem.at[1, g])
-        )
-        results[-1].start()
+        pltpu.make_async_copy(prior.at[g], prior_hbm.at[:, :, lanes(g)], out_sem.at[1]).start()
 
     mine_rows = pl.ds(pl.multiple_of(me * start_row, 8), H)
     other_rows = pl.ds(pl.multiple_of((1 - me) * start_row, 8), H)
@@ -387,6 +376,8 @@
     def group_at(j):
         dy, dx = groups[j]
         return ((y + dy) % Y) * X + (x + dx) % X
+
+    turn = [*range(1, Z), 0]
 
     def forward(first, end):
         total_rows = operator.shape[1]
@@ -414,63 +405,60 @@
                     wide[g, k // Z, k % Z, pl.ds(pair, rest)] = jnp.zeros(
                         (rest, LANES), jnp.float32
                     )
-            for j in range(len(groups)):
-                k = group_at(j)
+            for d in range(Z):
+                zz = (z + turn[d]) % Z
                 send(
-                    wide.at[g, k, :, other_rows], sib_in.at[g, k], rs_s.at[g, j], rs_r.at[g, j],
+                    wide.at[g, :, zz, other_rows], sib_in.at[g, :, zz], rs_s.at[g], rs_r.at[g, d],
                     sib,
                 )
+            sent(sib_in.at[g], rs_s.at[g])
 
     def pair_sum(g, j, zz):
         k = group_at(j)
         return wide[g, k, zz, mine_rows] + sib_in[g, k, zz]
 
-    turn = [*range(1, Z), 0]
-
     def scatter_xy(g):
-        for j, peer in enumerate(xy_peers):
-            k = group_at(j)
-            arrived(sib_in.at[g, k], rs_s.at[g, j], rs_r.at[g, j])
-            for d in range(Z):
-                value = pair_sum(g, j, (z + turn[d]) % Z)
+        for d in range(Z):
+            zz = (z + turn[d]) % Z
+            arrived(sib_in.at[g, :, zz], rs_r.at[g, d])
+            for j, peer in enumerate(xy_peers):
+                value = pair_sum(g, j, zz)
                 top = top_of(value, (0,))
-                xy_q[g, j, d] = coded(value, top)
-                xy_c[g, j, pl.ds(d, 1)] = top * (1.0 / LEVELS)
-            send(xy_c.at[g, j], xy_f.at[g, j], rc_s.at[g, j], rc_r.at[g, j], peer)
+                xy_q[g, d, j] = coded(value, top)
+                xy_c[g, d, j] = top * (1.0 / LEVELS)
+                send(xy_q.at[g, d, j], xy_r.at[g, d, j], rq_s.at[g], rq_r.at[g, d], peer)
+                send(xy_c.at[g, d, j], xy_f.at[g, d, j], rc_s.at[g], rc_r.at[g, d], peer)
+        sent(xy_q.at[g], rq_s.at[g])
+        sent(xy_c.at[g], rc_s.at[g])
+
+    def scatter_z(g):
         for d in range(Z):
-            for j, peer in enumerate(xy_peers):
-                send(
-                    xy_q.at[g, j, d], xy_r.at[g, j, d], rq_s.at[g, j, d], rq_r.at[g, j, d], peer
-                )
-
-    def scatter_z(g):
-        j = len(xy_peers)
-        arrived(sib_in.at[g, group_at(j)], rs_s.at[g, j], rs_r.at[g, j])
-        for i in range(j):
-            arrived(xy_f.at[g, i], rc_s.at[g, i], rc_r.at[g, i])
-        for d in range(Z):
-            value = pair_sum(g, j, (z + turn[d]) % Z)
-            for i in range(j):
-                arrived(xy_r.at[g, i, d], rq_s.at[g, i, d], rq_r.at[g, i, d])
-                value = value + decoded(xy_r[g, i, d], xy_f[g, i, pl.ds(d, 1)])
+            value = pair_sum(g, len(xy_peers), (z + turn[d]) % Z)
+            arrived(xy_r.at[g, d], rq_r.at[g, d])
+            arrived(xy_f.at[g, d], rc_r.at[g, d])
+            for i in range(len(xy_peers)):
+                value = value + decoded(xy_r[g, d, i], xy_f[g, d, i])
             if d == Z - 1:
                 own[g] = value
                 break
             top = top_of(value, (0,))
             z_q[g, d] = coded(value, top)
-            z_c[g, d] = jnp.broadcast_to(top * (1.0 / LEVELS), (8, LANES))
-            send(z_c.at[g, d], z_f.at[g, d], zc_s.at[g, d], zc_r.at[g, d], z_peers[d])
-            send(z_q.at[g, d], z_r.at[g, d], zq_s.at[g, d], zq_r.at[g, d], z_peers[d])
+            z_c[g, d] = top * (1.0 / LEVELS)
+            send(z_q.at[g, d], z_r.at[g, d], zq_s.at[g], zq_r.at[g], z_peers[d])
+            send(z_c.at[g, d], z_f.at[g, d], zc_s.at[g], zc_r.at[g], z_peers[d])
+        if Z > 1:
+            sent(z_q.at[g], zq_s.at[g])
+            sent(z_c.at[g], zc_s.at[g])
 
     def scatter_end(g):
         value = own[g]
+        if Z > 1:
+            arrived(z_r.at[g], zq_r.at[g])
+            arrived(z_f.at[g], zc_r.at[g])
         for d in range(1, Z):
-            arrived(z_r.at[g, d - 1], zq_s.at[g, d - 1], zq_r.at[g, d - 1])
-            arrived(z_f.at[g, d - 1], zc_s.at[g, d - 1], zc_r.at[g, d - 1])
-            value = value + decoded(z_r[g, d - 1], z_f[g, d - 1][:1])
+            value = value + decoded(z_r[g, d - 1], z_f[g, d - 1])
         out[g] = value
-        results.append(pltpu.make_async_copy(out.at[g], out_hbm.at[:, lanes(g)], out_sem.at[0, g]))
-        results[-1].start()
+        pltpu.make_async_copy(out.at[g], out_hbm.at[:, lanes(g)], out_sem.at[0]).start()
 
     class_sides()
     for g in range(chunks):
@@ -492,7 +480,7 @@
     halo_recv(0)
     for g in range(chunks):
         halo_sides(g)
-        sweeps(g, {2: functools.partial(scatter_xy, g - 1)} if g else {})
+        sweeps(g, {m // 2 + 1: functools.partial(scatter_xy, g - 1)} if g else {})
         if g + 1 < chunks:
             halo_recv(g + 1)
         forward(g, g + 1)
@@ -506,8 +494,8 @@
         scatter_end(g)
     scatter_z(last)
     scatter_end(last)
-    for copy in results:
-        copy.wait()
+    pltpu.make_async_copy(prior_hbm, prior_hbm, out_sem.at[1]).wait()
+    pltpu.make_async_copy(out_hbm, out_hbm, out_sem.at[0]).wait()
     for has, copy in pending:
         if has is None:
             copy.wait_send()
@@ -537,8 +525,10 @@
     def vmem(*shape, kind=f32):
         return pltpu.VMEM(shape, kind)
 
-    def sems(*shape):
-        return [pltpu.SemaphoreType.DMA(shape)] * 2
+    dma = pltpu.SemaphoreType.DMA
+
+    def sems(*shapes):
+        return [dma(shape) for shape in shapes]
 
     field = (rows + 2 * m, cols + 2 * m)
     even = 2 * count % 8 == 0
@@ -561,39 +551,39 @@
         vmem(*field, LANES),
         vmem(*field, LANES),
         vmem(chunks, rows, cols, LANES, kind=i16),
-        vmem(chunks, 8, LANES),
+        vmem(chunks, 1, LANES),
         vmem(chunks, 2, m, cols, LANES, kind=i16),
-        vmem(chunks, 2, 8, LANES),
+        vmem(chunks, 2, 1, LANES),
         vmem(points, width, kind=bf16),
         vmem(*((8,) if even else (data_rows,)), LANES),
         vmem(chunks, Y * X, Z, tall, LANES),
         vmem(chunks, Y * X, Z, H, LANES),
-        vmem(chunks, peers, Z, H, LANES, kind=i16),
-        vmem(chunks, peers, Z, LANES),
-        vmem(chunks, peers, Z, H, LANES, kind=i16),
-        vmem(chunks, peers, Z, LANES),
+        vmem(chunks, Z, peers, H, LANES, kind=i16),
+        vmem(chunks, Z, peers, 1, LANES),
+        vmem(chunks, Z, peers, H, LANES, kind=i16),
+        vmem(chunks, Z, peers, 1, LANES),
         vmem(chunks, zs, H, LANES, kind=i16),
-        vmem(chunks, zs, 8, LANES),
+        vmem(chunks, zs, 1, LANES),
         vmem(chunks, zs, H, LANES, kind=i16),
-        vmem(chunks, zs, 8, LANES),
+        vmem(chunks, zs, 1, LANES),
         vmem(chunks, H, LANES),
-        pltpu.SemaphoreType.DMA,
-        pltpu.SemaphoreType.DMA((3,)),
-        pltpu.SemaphoreType.DMA((2, chunks)),
-        pltpu.SemaphoreType.DMA((chunks,)),
-        *sems(4),
-        *sems(chunks, zs),
-        *sems(chunks, Z, peers),
-        *sems(chunks, peers + 1),
-        *sems(chunks, 2),
-        *sems(chunks, 2),
-        *sems(chunks, 2),
-        *sems(chunks, 2, 2),
-        *sems(chunks, peers + 1),
-        *sems(chunks, peers, Z),
-        *sems(chunks, peers),
-        *sems(chunks, zs),
-        *sems(chunks, zs),
+        dma,
+        dma((3,)),
+        dma((2,)),
+        dma,
+        dma((4,)),
+        dma((4,)),
+        *sems((chunks,), (chunks, zs)),
+        *sems((chunks, peers), (chunks, peers)),
+        *sems((chunks,), (chunks,)),
+        *sems((chunks, 2), (chunks, 2)),
+        *sems((chunks, 2), (chunks, 2)),
+        *sems((chunks, 2), (chunks, 2)),
+        *sems((chunks,), (chunks, Z)),
+        *sems((chunks,), (chunks, Z)),
+        *sems((chunks,), (chunks, Z)),
+        *sems((chunks,), (chunks,)),
+        *sems((chunks,), (chunks,)),
     ]
     anywhere = pl.BlockSpec(memory_space=pl.ANY)
     hbm = pl.BlockSpec(memory_space=pltpu.HBM)

time: 63.5 us -> 61.3 us (0.965)
  Pallas kernels: 60.8 us -> 58.6 us
    pallas_call x1, Pallas kernels: 60.8 us -> 58.6 us  [local(): pl.pallas_call(functools.partial(block_kernel, (Y, X, Z), (gx_size, gy_si...]
where the time goes in v3:
time: 61.3 us; the launch traced here: 61.1 us
  Pallas kernels  58.6 us (96%)
  local copies, waits for them, and re-layouts  1.15 us (2%)
  other arithmetic  0.73 us (1%)
  between operations  0.69 us (1%)
    pallas_call x1, Pallas kernels, local(): pl.pallas_call(functools.partial(block_kernel, (Y, X, Z), (gx_size, gy_si...  58.6 us

profile of v3, /device:TPU:0, one launch (start us, length us, event | category | flops | bytes accessed | tf_op | source)
XLA Modules:
  0.0 61.1 jit_solution(13516268841823937701)
XLA Ops:
  0.6 0.0 copy-start
  0.7 0.0 copy-start.1
  0.7 58.6 %shard_map.77 = (f32[80,384]{1,0:T(8,128)S(1)}, f32[16,64,384]{2,1,0:T(8,128)S(1)}) custom-call(bf16[76,384]{1,0:T(8,128)(2,1)} %mine.1, s32[16,64]{1,0:T(8,128)} %class_map.1, f32[16]{0:T(128)} %diffusion_hbm.1, f32[16]{0:T(128)} %kappa_hbm.1, bf16[1024,2432]{1,0:T(8,128)(2,1)} %bitcast.1), custom_call_target="tpu_custom_call" | custom-call | tf_op jit(solution)/shard_map/pallas_call | solution.py:590
  59.2 0.0 copy-done
  59.3 0.0 copy-done.1
  59.3 0.7 %multiply_add_fusion = f32[76,384]{1,0:T(8,128)} fusion(bf16[76,384]{1,0:T(8,128)(2,1)S(1)} %copy-done, f32[80,384]{1,0:T(8,128)S(1)} %get-tuple-element.4, f32[76]{0:T(128)S(1)} %copy-done.1, pred[]{:T(512)S(6)} %eq.5), kind=kLoop, calls=%fused_computation | loop fusion | flops 116736 | bytes 408881 | tf_op jit(solution)/shard_map/add | solution.py:605
  60.0 1.1 %copy.9 = f32[16,64,384]{2,1,0:T(8,128)} copy(f32[16,64,384]{2,1,0:T(8,128)S(1)} %get-tuple-element.9) | data formatting | bytes 3145728
Async XLA Ops:
  0.6 58.6 %copy-start = (bf16[76,384]{1,0:T(8,128)(2,1)S(1)}, bf16[76,384]{1,0:T(8,128)(2,1)}, u32[]{:S(2)}) copy-start(bf16[76,384]{1,0:T(8,128)(2,1)} %mine.1) | copy-start | bytes 175108
  0.7 58.6 %copy-start.1 = (f32[76]{0:T(128)S(1)}, f32[76]{0:T(128)}, u32[]{:S(2)}) copy-start(f32[76]{0:T(128)} %param.8) | copy-start | bytes 916

commit v4 on v3

--- a/solution.py
+++ b/solution.py
@@ -39,7 +39,7 @@
     mine, class_map, diffusion_hbm, kappa_hbm, operator_hbm,
     out_hbm, prior_hbm,
     out, prior, class_in, diffusion_table, kappa_table, operator, classes, thin, full, stage, data, near_classes, coef, inverse,
-    s, u, v, q_out, q_scale, q_in, q_in_scale, smooth,
+    s, fixed, u, v, line, q_out, q_scale, q_in, q_in_scale, smooth,
     flat, wide, sib_in, xy_q, xy_c, xy_r, xy_f, z_q, z_c, z_r, z_f, own,
     op_sem, in_sem, out_sem, own_sem, cls_s, cls_r, gz_s, gz_r, gx_s, gx_r, gs_s, gs_r,
     hq_s, hq_r, hc_s, hc_r, he_s, he_r,
@@ -223,17 +223,24 @@
             )
             return padded.T
 
-        for i, w in enumerate(weights):
-            thin[i] = upright(jnp.where(inside, w / divisor, 0.0))
-        turned = upright(1.0 / divisor)
+        scale = 1.0 / jnp.sqrt(divisor)
+        present = jnp.where(inside, scale, 0.0)
+        for i, (w, shift, axis) in enumerate(
+            ((weights[1], tall - 1, 0), (weights[3], LANES - 1, 1))
+        ):
+            thin[i] = upright(w * present * pltpu.roll(present, shift, axis))
+        turned = upright(scale)
         for r in range(rows):
             inverse[r] = jnp.broadcast_to(turned[m : m + cols, m + r : m + r + 1], (cols, LANES))
 
 
+    parts = wide_cols // 8
+
     def coefficient(i):
-        turned = thin[i]
-        for r in range(wide_rows):
-            coef[i, r] = jnp.broadcast_to(turned[:wide_cols, r : r + 1], (wide_cols, LANES))
+        for j in range(parts):
+            turned = thin[i, pl.ds(j, 8, parts), :]
+            for r in range(wide_rows):
+                coef[i, r, j] = jnp.broadcast_to(turned[:, r : r + 1], (8, LANES))
 
     def held(g, d, core=me):
         return full.at[g, y, x, core, (z - d) % Z]
@@ -338,9 +345,20 @@
             def _():
                 arrived(s.at[g, strip, pl.ds(dst, m)], he_r.at[g, i])
 
+    def westward(row):
+        return jnp.concatenate([pltpu.roll(row[parts - 1 :], 1, 1), row[: parts - 1]], axis=0)
+
+    def eastward(row):
+        return jnp.concatenate([row[1:], pltpu.roll(row[:1], 7, 1)], axis=0)
+
     def sweeps(g, hooks):
         turns = [u, v]
-        fixed = s.at[g]
+
+        @pl.loop(0, wide_rows)
+        def _(r):
+            for j in range(parts):
+                fixed[r, j] = s[g, r, pl.ds(j, 8, parts)]
+
         for step in range(1, m + 1):
             if step in hooks:
                 hooks[step]()
@@ -348,24 +366,31 @@
             new = turns[(step + 1) % 2]
             last = step == m
 
-            def swept(r):
-                centre = old[r]
-                value = fixed[r] + coef[0, r] * old[r - 1]
-                value = value + coef[1, r] * old[r + 1]
-                value = value + coef[2, r] * pltpu.roll(centre, 1, 0)
-                value = value + coef[3, r] * pltpu.roll(centre, wide_cols - 1, 0)
-                if last:
-                    done = value[m : m + cols]
-                    prior[g, r - m] = done
-                    at = pl.multiple_of((r - m) * cols, cols)
-                    smooth[pl.ds(at, cols), lanes(g)] = done.astype(jnp.bfloat16)
-                else:
-                    new[r] = value
-
-            @pl.loop(0, (wide_rows - 2 * step) // 2)
-            def _(i):
-                swept(step + 2 * i)
-                swept(step + 2 * i + 1)
+            def pair_of_rows(i, carry, step=step, old=old, new=new, last=last):
+                flux, centre = carry
+                for k in (0, 1):
+                    r = step + 2 * i + k
+                    down, right, below = coef[0, r], coef[1, r], old[r + 1]
+                    value = fixed[r] + flux
+                    value = value + down * below
+                    value = value + westward(right * centre)
+                    value = value + right * eastward(centre)
+                    flux, centre = down * centre, below
+                    if last:
+                        for j in range(parts):
+                            line[k, pl.ds(j, 8, parts)] = value[j]
+                        done = line[k, pl.ds(m, cols)] * inverse[r - m]
+                        prior[g, r - m] = done
+                        at = pl.multiple_of((r - m) * cols, cols)
+                        smooth[pl.ds(at, cols), lanes(g)] = done.astype(jnp.bfloat16)
+                    else:
+                        new[r] = value
+                return flux, centre
+
+            lax.fori_loop(
+                0, (wide_rows - 2 * step) // 2, pair_of_rows,
+                (coef[0, step - 1] * old[step - 1], old[step]),
+            )
 
         pltpu.make_async_copy(prior.at[g], prior_hbm.at[:, :, lanes(g)], out_sem.at[1]).start()
 
@@ -382,13 +407,10 @@
     def forward(first, end):
         total_rows = operator.shape[1]
         cut = -(-total_rows // 2 // LANES) * LANES
-        right = smooth[:, first * LANES : end * LANES]
+        left = smooth[:, first * LANES : end * LANES].T
         partial = jnp.concatenate(
             [
-                lax.dot_general(
-                    operator[:, part], right, (((0,), (0,)), ((), ())),
-                    preferred_element_type=jnp.float32,
-                )
+                jnp.dot(left, operator[:, part], preferred_element_type=jnp.float32).T
                 for part in (pl.ds(0, cut), pl.ds(cut, total_rows - cut))
             ],
             axis=0,
@@ -465,35 +487,36 @@
         gather_z(g)
         if g == 0:
             coefficients()
-        else:
+    load.wait()
+    for g in range(chunks):
+        gather_xy(g)
+        if g in (1, 2):
             coefficient(g - 1)
-    for i in range(chunks - 1, 4):
-        coefficient(i)
-    load.wait()
-    gather_xy(0)
-    sib_blocks(0)
-    sources(0, 1)
-    for g in range(1, chunks):
-        gather_xy(g)
+        if g == chunks - 1 and g:
+            halo_recv(0)
         sib_blocks(g)
         sources(g, g + 1)
-    halo_recv(0)
+    for i in range(chunks - 1, 2):
+        coefficient(i)
+    if chunks == 1:
+        halo_recv(0)
     for g in range(chunks):
         halo_sides(g)
-        sweeps(g, {m // 2 + 1: functools.partial(scatter_xy, g - 1)} if g else {})
+        hooks = {}
+        if g:
+            hooks[m // 2 + 1] = functools.partial(scatter_xy, g - 1)
         if g + 1 < chunks:
-            halo_recv(g + 1)
+            hooks[m - 1] = functools.partial(halo_recv, g + 1)
+        sweeps(g, hooks)
         forward(g, g + 1)
     last = chunks - 1
     for g in range(last - 1):
         scatter_z(g)
     scatter_xy(last)
-    for g in range(max(last - 1, 0), last):
+    for g in range(max(last - 1, 0), chunks):
         scatter_z(g)
-    for g in range(last):
+    for g in range(chunks):
         scatter_end(g)
-    scatter_z(last)
-    scatter_end(last)
     pltpu.make_async_copy(prior_hbm, prior_hbm, out_sem.at[1]).wait()
     pltpu.make_async_copy(out_hbm, out_hbm, out_sem.at[0]).wait()
     for has, copy in pending:
@@ -531,6 +554,7 @@
         return [dma(shape) for shape in shapes]
 
     field = (rows + 2 * m, cols + 2 * m)
+    strided = (field[0], field[1] // 8, 8, LANES)
     even = 2 * count % 8 == 0
     scratch = [
         vmem(chunks, H, LANES),
@@ -540,16 +564,18 @@
         pltpu.SMEM(kappa_table.shape, f32),
         vmem(points, data_rows, kind=bf16),
         vmem(3, rows, LANES, kind=i32),
-        vmem(4, LANES, LANES),
+        vmem(2, LANES, LANES),
         vmem(chunks, Y, X, 2, Z, count, LANES, kind=bf16),
         vmem(data_rows, LANES),
         vmem(data_rows, width, kind=bf16),
         vmem(2, 3, rows, LANES, kind=i32),
-        vmem(4, *field, LANES),
+        vmem(2, *strided),
         vmem(rows, cols, LANES),
         vmem(chunks, *field, LANES),
-        vmem(*field, LANES),
-        vmem(*field, LANES),
+        vmem(*strided),
+        vmem(*strided),
+        vmem(*strided),
+        vmem(2, field[1], LANES),
         vmem(chunks, rows, cols, LANES, kind=i16),
         vmem(chunks, 1, LANES),
         vmem(chunks, 2, m, cols, LANES, kind=i16),

time: 61.3 us -> 58 us (0.946)
  Pallas kernels: 58.6 us -> 55.3 us
    pallas_call x1, Pallas kernels: 58.6 us -> 55.3 us  [local(): pl.pallas_call(functools.partial(block_kernel, (Y, X, Z), (gx_size, gy_si...]
where the time goes in v4:
time: 58 us; the launch traced here: 57.8 us
  Pallas kernels  55.3 us (95%)
  local copies, waits for them, and re-layouts  1.15 us (2%)
  other arithmetic  0.73 us (1%)
  between operations  0.69 us (1%)
    pallas_call x1, Pallas kernels, local(): pl.pallas_call(functools.partial(block_kernel, (Y, X, Z), (gx_size, gy_si...  55.3 us

profile of v4, /device:TPU:0, one launch (start us, length us, event | category | flops | bytes accessed | tf_op | source)
XLA Modules:
  0.0 57.8 jit_solution(15399523924156747433)
XLA Ops:
  0.6 0.0 copy-start
  0.7 0.0 copy-start.1
  0.7 55.3 %shard_map.77 = (f32[80,384]{1,0:T(8,128)S(1)}, f32[16,64,384]{2,1,0:T(8,128)S(1)}) custom-call(bf16[76,384]{1,0:T(8,128)(2,1)} %mine.1, s32[16,64]{1,0:T(8,128)} %class_map.1, f32[16]{0:T(128)} %diffusion_hbm.1, f32[16]{0:T(128)} %kappa_hbm.1, bf16[1024,2432]{1,0:T(8,128)(2,1)} %bitcast.1), custom_call_target="tpu_custom_call" | custom-call | tf_op jit(solution)/shard_map/pallas_call | solution.py:616
  55.9 0.0 copy-done
  56.0 0.0 copy-done.1
  56.0 0.7 %multiply_add_fusion = f32[76,384]{1,0:T(8,128)} fusion(bf16[76,384]{1,0:T(8,128)(2,1)S(1)} %copy-done, f32[80,384]{1,0:T(8,128)S(1)} %get-tuple-element.4, f32[76]{0:T(128)S(1)} %copy-done.1, pred[]{:T(512)S(6)} %eq.5), kind=kLoop, calls=%fused_computation | loop fusion | flops 116736 | bytes 408881 | tf_op jit(solution)/shard_map/add | solution.py:631
  56.7 1.1 %copy.9 = f32[16,64,384]{2,1,0:T(8,128)} copy(f32[16,64,384]{2,1,0:T(8,128)S(1)} %get-tuple-element.9) | data formatting | bytes 3145728
Async XLA Ops:
  0.6 55.3 %copy-start = (bf16[76,384]{1,0:T(8,128)(2,1)S(1)}, bf16[76,384]{1,0:T(8,128)(2,1)}, u32[]{:S(2)}) copy-start(bf16[76,384]{1,0:T(8,128)(2,1)} %mine.1) | copy-start | bytes 175108
  0.7 55.3 %copy-start.1 = (f32[76]{0:T(128)S(1)}, f32[76]{0:T(128)}, u32[]{:S(2)}) copy-start(f32[76]{0:T(128)} %param.8) | copy-start | bytes 916
